TPU v7x, 512 devices: a whole 4x8x8 slice. The times are simulated.
512 devices in a mesh: gx: 16 (over y_lo, x), gy: 16 (over z, y_hi), col: 2 (over core).
Axes of the slice: x: 4, y: 8 (y_hi: 2, y_lo: 4; y = y_hi * 4 + y_lo), z: 8, core: 2. Of those that a mesh axis runs over, the one named last changes fastest.
Arguments:
- density: float32 [10, 10, 10, 64, 2048], P('col', None, None, 'gx', 'gy'), may hold values from -6 to 6
- velocity: float32 [2, 64, 2048], P(None, 'gx', 'gy'), may hold values from -3 to 3
- shear_rates: float32 [4, 64, 2048], P(None, 'gx', 'gy'), may hold values from -4 to 4
- hermite_matrix: float32 [10, 10], replicated, may hold values from -2 to 2
- laguerre_matrix: float32 [10, 10], replicated, may hold values from -2 to 2
- flow_first: float32 [4, 10, 10], replicated, may hold values from -2 to 2
- flow_second: float32 [4, 10, 10], replicated, may hold values from -2 to 2
- stress_weights: float32 [3, 10, 10, 10], P(None, 'col'), may hold values from -0.1875 to 0.1875
Outputs:
- advanced: float32 [10, 10, 10, 64, 2048], P('col', None, None, 'gx', 'gy')
- stress: float32 [3, 64, 2048], P(None, 'gx', 'gy')
All inputs are finite; a program needn't handle non-finite values.
Results may differ from a plain program's by a relative error of at most 0.0003.
Values sent between devices are 32-bit elements; how exact they have to be, the bound alone decides.
No kernel may reach another device: no remote copies, remote signals or barrier semaphores. Data moves between devices by JAX's collectives and lax.ppermute only.
A program may use at most 128 MiB of HBM per device.

v0:
```python
import functools

import jax
import jax.numpy as jnp
from jax import lax
from jax.experimental import pallas as pl
from jax.experimental.pallas import tpu as pltpu
from jax.sharding import PartitionSpec as P

time_step = 0.1
highest = lax.Precision.HIGHEST
f32 = jnp.float32
bf16 = jnp.bfloat16

ROWS = 2000
PQ = 50
RX = 40
PQ_PAD = 56
K_HALF = 64
N_PAIR = 20
MODES_P = 100
MODES_PAD = 104


def upwind(speed):
    plus = jnp.maximum(speed, 0.0)
    minus = jnp.minimum(speed, 0.0)
    t = time_step
    center = (-1.5 * t) * jnp.abs(speed)
    return center, (2 * t) * plus, (-0.5 * t) * plus, (-2 * t) * minus, (0.5 * t) * minus


def tens(value):
    total = jnp.zeros_like(value)
    for j in range(1, 5):
        total = total + (value >= 10 * j).astype(jnp.int32)
    return total


def iota(shape, dim):
    return lax.broadcasted_iota(jnp.int32, shape, dim)


def one_hot(condition):
    return jnp.where(condition, 1.0, 0.0).astype(f32)


def halo_kernel(x_ref, low_ref, high_ref):
    for k in range(2):
        low_ref[0, k, 0:MODES_P, :] = x_ref[pl.ds(k, MODES_P, stride=4), :]
        high_ref[0, k, 0:MODES_P, :] = x_ref[pl.ds(2 + k, MODES_P, stride=4), :]


def x_halos(rows):
    shape = jax.ShapeDtypeStruct((5, 2, MODES_PAD, 128), f32)
    spec = pl.BlockSpec((1, 2, MODES_PAD, 128), lambda p: (p, 0, 0, 0))
    return pl.pallas_call(
        halo_kernel,
        grid=(5,),
        in_specs=[pl.BlockSpec((400, 128), lambda p: (p, 0))],
        out_specs=[spec, spec],
        out_shape=[shape, shape],
        cost_estimate=pl.CostEstimate(flops=0, bytes_accessed=2 * ROWS * 512, transcendentals=0),
        name="x_halos",
    )(rows)


def edge_kernel(x_ref, low_ref, high_ref, rows_ref):
    rows_ref[96:128, :] = jnp.zeros((32, 128), f32)
    lane = iota((8, 128), 1)
    row = iota((8, 128), 0)
    pick = one_hot(((row < 2) & (lane == row)) | ((row >= 2) & (row < 4) & (lane == row + 124)))
    for x in range(4):
        rows_ref[0:MODES_P, :] = x_ref[pl.ds(x, MODES_P, stride=4), :]
        edges = lax.dot_general(
            pick, rows_ref[...], (((1,), (1,)), ((), ())), precision=highest, preferred_element_type=f32
        )
        low_ref[:, x * 128 : (x + 1) * 128] = edges[0:2]
        high_ref[:, x * 128 : (x + 1) * 128] = edges[2:4]


def y_edges(rows):
    shape = jax.ShapeDtypeStruct((2, 5 * 512), f32)
    spec = pl.BlockSpec((2, 512), lambda p: (0, p))
    return pl.pallas_call(
        edge_kernel,
        grid=(5,),
        in_specs=[pl.BlockSpec((400, 128), lambda p: (p, 0))],
        out_specs=[spec, spec],
        out_shape=[shape, shape],
        scratch_shapes=[pltpu.VMEM((128, 128), f32)],
        cost_estimate=pl.CostEstimate(flops=0, bytes_accessed=ROWS * 512, transcendentals=0),
        name="y_edges",
    )(rows)


def split(value):
    high = value.astype(bf16)
    low = (value - high.astype(f32)).astype(bf16)
    return high, low


def coupling(start, first, second, hermite):
    rows = 5 * PQ_PAD

    def row_ids(width):
        i = iota((rows, width), 0)
        c = jnp.zeros_like(i)
        for j in range(1, 5):
            c = c + (i >= PQ_PAD * j).astype(jnp.int32)
        ab = i - PQ_PAD * c
        a = tens(ab)
        return c, a + start, ab - 10 * a, ab < PQ

    def expand(table, index, c, valid):
        t40 = iota((rows, 40), 1)
        t10 = iota((rows, 10), 1)
        c40, a40, b40, ok40 = row_ids(40)
        c10, a10, b10, ok10 = row_ids(10)
        i40 = a40 if index == 0 else b40
        i10 = a10 if index == 0 else b10
        pick_flow = one_hot(ok40 & (c40 < 4) & (t40 == 4 * i40 + c40))
        pick_spring = one_hot(ok10 & (c10 == 4) & (t10 == i10))
        return jnp.dot(pick_flow, table, precision=highest, preferred_element_type=f32) + jnp.dot(
            pick_spring, hermite, precision=highest, preferred_element_type=f32
        )

    def columns(height):
        k = iota((height, 128), 1)
        other = k >= K_HALF
        kk = jnp.where(other, k - K_HALF, k)
        p_here = tens(kk)
        p = p_here + jnp.where(other, 5 - start, start)
        return p, kk - 10 * p_here, kk < PQ

    c, a, b, valid = row_ids(128)
    p10, q10, ok10 = columns(10)
    source = iota((10, 128), 0)
    left = expand(first, 0, c, valid)
    right = expand(second, 1, c, valid)
    left = jnp.dot(left, one_hot(ok10 & (source == p10)), precision=highest, preferred_element_type=f32)
    right = jnp.dot(right, one_hot(ok10 & (source == q10)), precision=highest, preferred_element_type=f32)
    p, q, ok = columns(rows)
    spring = c == 4
    both = left * jnp.where(spring, one_hot(b == q), right)
    both = both + jnp.where(spring & (a == p), right, 0.0)
    return time_step * both


def main_kernel(
    place_ref,
    laguerre_ref,
    own_hbm,
    other_hbm,
    velocity_ref,
    shear_ref,
    first_ref,
    second_ref,
    hermite_ref,
    out_hbm,
    own_ref,
    other_ref,
    turned_ref,
    rate_ref,
    result_ref,
    wide_ref,
    narrow_ref,
    coef_ref,
    sems,
):
    copy_own = pltpu.make_async_copy(own_hbm, own_ref.at[0:ROWS], sems.at[0])
    copy_other = pltpu.make_async_copy(other_hbm, other_ref.at[0:ROWS], sems.at[1])
    copy_own.start()
    copy_other.start()
    zeros = jnp.zeros((K_HALF * RX - ROWS, 128), f32)
    own_ref[ROWS:, :] = zeros
    other_ref[ROWS:, :] = zeros

    matrix = coupling(place_ref[0], first_ref[...], second_ref[...], hermite_ref[...])
    matrix_high, matrix_low = split(matrix)
    wide_ref[:, 0:128] = matrix_high
    wide_ref[:, 128:256] = matrix_high
    narrow_ref[...] = matrix_low

    u = velocity_ref[0:4, :]
    v = velocity_ref[4:8, :]
    lane = iota((4, 128), 1)
    u0, um1, um2, up1, up2 = upwind(u)
    v0, vm1, vm2, vp1, vp2 = upwind(v)
    coefs = (
        1.0 + u0 + v0,
        um1,
        um2,
        up1,
        up2,
        jnp.where(lane >= 1, vm1, 0.0),
        jnp.where(lane >= 2, vm2, 0.0),
        jnp.where(lane < 127, vp1, 0.0),
        jnp.where(lane < 126, vp2, 0.0),
    )
    for i, c in enumerate(coefs):
        coef_ref[i, 0:4, :] = c

    copy_own.wait()
    copy_other.wait()

    def pair(i, carry):
        parts = []
        for t in range(2):
            rx = 2 * i + t
            own = own_ref[pl.ds(rx, K_HALF, stride=RX), :]
            other = other_ref[pl.ds(rx, K_HALF, stride=RX), :]
            turned_ref[pl.ds(pl.multiple_of(rx * K_HALF, K_HALF), K_HALF), :] = own
            own_high, own_low = split(own)
            other_high, other_low = split(other)
            parts.append(jnp.concatenate([own_high, other_high, own_low, other_low], axis=0))
        data = jnp.concatenate(parts, axis=1)
        product = jnp.dot(wide_ref[...], data, preferred_element_type=f32)
        product = product + jnp.dot(narrow_ref[...], data[0:128], preferred_element_type=f32)
        for t in range(2):
            rx = 2 * i + t
            x = lax.rem(rx, 4)
            part = product[:, t * 128 : (t + 1) * 128]
            total = part[4 * PQ_PAD : 5 * PQ_PAD]
            for c in range(4):
                total = total + shear_ref[pl.ds(4 * c + x, 1), :] * part[c * PQ_PAD : (c + 1) * PQ_PAD]
            rate_ref[pl.ds(pl.multiple_of(rx * PQ_PAD, PQ_PAD), PQ_PAD), :] = total
        return carry

    lax.fori_loop(0, N_PAIR, pair, 0)

    def strip(j, carry):
        def field(r, x):
            return turned_ref[pl.ds(pl.multiple_of((4 * r + x) * K_HALF + 8 * j, 8), 8), :]

        for x in range(4):
            def coef(i):
                return coef_ref[i, x : x + 1, :]

            here = [field(r, x) for r in range(10)]
            for r in range(10):
                mixed = laguerre_ref[r, 0] * here[0]
                for s in range(1, 10):
                    mixed = mixed + laguerre_ref[r, s] * here[s]
                f = here[r]
                total = rate_ref[pl.ds(pl.multiple_of((4 * r + x) * PQ_PAD + 8 * j, 8), 8), :]
                total = total + time_step * mixed + coef(0) * f
                for shift, i in ((-1, 1), (-2, 2), (1, 3), (2, 4)):
                    if 0 <= x + shift < 4:
                        total = total + coef(i) * field(r, x + shift)
                for shift, i in ((1, 5), (2, 6), (127, 7), (126, 8)):
                    total = total + coef(i) * pltpu.roll(f, shift, 1)
                result_ref[pl.ds(j * (8 * RX) + 4 * r + x, 8, stride=RX), :] = total
        return carry

    lax.fori_loop(0, PQ_PAD // 8, strip, 0)
    copy_out = pltpu.make_async_copy(result_ref.at[0:ROWS], out_hbm, sems.at[2])
    copy_out.start()
    copy_out.wait()


def main(place, laguerre, own, other, velocity, shear, first, second, hermite):
    vmem = pl.BlockSpec(memory_space=pltpu.VMEM)
    smem = pl.BlockSpec(memory_space=pltpu.SMEM)
    hbm = pl.BlockSpec(memory_space=pl.ANY)
    return pl.pallas_call(
        main_kernel,
        in_specs=[smem, smem, hbm, hbm, vmem, vmem, vmem, vmem, vmem],
        out_specs=hbm,
        out_shape=jax.ShapeDtypeStruct((ROWS, 128), f32),
        scratch_shapes=[
            pltpu.VMEM((K_HALF * RX, 128), f32),
            pltpu.VMEM((K_HALF * RX, 128), f32),
            pltpu.VMEM((K_HALF * RX, 128), f32),
            pltpu.VMEM((PQ_PAD * RX, 128), f32),
            pltpu.VMEM((PQ_PAD * RX, 128), f32),
            pltpu.VMEM((5 * PQ_PAD, 256), bf16),
            pltpu.VMEM((5 * PQ_PAD, 128), bf16),
            pltpu.VMEM((9, 8, 128), f32),
            pltpu.SemaphoreType.DMA((3,)),
        ],
        compiler_params=pltpu.CompilerParams(vmem_limit_bytes=24 << 20),
        cost_estimate=pl.CostEstimate(flops=2 * 280 * 384 * 5120, bytes_accessed=3 * ROWS * 512, transcendentals=0),
        name="main_step",
    )(place, laguerre, own, other, velocity, shear, first, second, hermite)


def final_kernel(
    partial_ref, left_ref, right_ref, below_ref, above_ref, velocity_ref, weight_ref, out_ref, stress_ref
):
    p = pl.program_id(0)
    u = velocity_ref[0:4, :]
    v = velocity_ref[4:8, :]
    lane4 = iota((4, 128), 1)
    _, um1, um2, up1, up2 = upwind(u)
    _, vm1, vm2, vp1, vp2 = upwind(v)
    near = jnp.where(lane4 == 0, vm1, jnp.where(lane4 == 127, vp1, 0.0))
    far = jnp.where(lane4 <= 1, vm2, jnp.where(lane4 >= 126, vp2, 0.0))

    edges = jnp.concatenate([below_ref[...], above_ref[...], jnp.zeros((4, 512), f32)], axis=0)
    high = edges.astype(bf16).astype(f32)
    rest = edges - high
    middle = rest.astype(bf16).astype(f32)
    low = rest - middle
    stacked = jnp.concatenate([high, middle, low, jnp.zeros((8, 512), f32)], axis=0).astype(bf16)
    row = lax.rem(iota((32, 256), 0), 8)
    lane = iota((32, 256), 1)
    hit = (row == 1) & ((lane == 0) | (lane == 129))
    hit = hit | ((row == 2) & ((lane == 127) | (lane == 254)))
    hit = hit | ((row == 0) & (lane == 128))
    hit = hit | ((row == 3) & (lane == 255))
    spread = lax.dot_general(
        stacked, one_hot(hit).astype(bf16), (((0,), (0,)), ((), ())), preferred_element_type=f32
    )

    @pl.when(p == 0)
    def _():
        stress_ref[...] = jnp.zeros_like(stress_ref)

    left_far = left_ref[0, 0, 0:MODES_P, :]
    left_near = left_ref[0, 1, 0:MODES_P, :]
    right_near = right_ref[0, 0, 0:MODES_P, :]
    right_far = right_ref[0, 1, 0:MODES_P, :]
    for x in range(4):
        total = partial_ref[pl.ds(x, MODES_P, stride=4), :]
        total = total + near[x : x + 1] * spread[x * 128 : x * 128 + MODES_P, 0:128]
        total = total + far[x : x + 1] * spread[x * 128 : x * 128 + MODES_P, 128:256]
        if x == 0:
            total = total + um1[0:1] * left_near + um2[0:1] * left_far
        if x == 1:
            total = total + um2[1:2] * left_near
        if x == 2:
            total = total + up2[2:3] * right_near
        if x == 3:
            total = total + up1[3:4] * right_near + up2[3:4] * right_far
        out_ref[pl.ds(x, MODES_P, stride=4), :] = total
        for s in range(3):
            moment = jnp.sum(weight_ref[0, :, s : s + 1] * total, axis=0, keepdims=True)
            stress_ref[4 * s + x : 4 * s + x + 1, :] += moment


def final(partial, left, right, below, above, velocity, weights):
    halo = pl.BlockSpec((1, 2, MODES_PAD, 128), lambda p: (p, 0, 0, 0))
    edge = pl.BlockSpec((2, 512), lambda p: (0, p))
    rows = pl.BlockSpec((400, 128), lambda p: (p, 0))
    return pl.pallas_call(
        final_kernel,
        grid=(5,),
        in_specs=[
            rows,
            halo,
            halo,
            edge,
            edge,
            pl.BlockSpec((8, 128), lambda p: (0, 0)),
            pl.BlockSpec((1, MODES_P, 3), lambda p: (p, 0, 0)),
        ],
        out_specs=[rows, pl.BlockSpec((12, 128), lambda p: (0, 0))],
        out_shape=[jax.ShapeDtypeStruct((ROWS, 128), f32), jax.ShapeDtypeStruct((12, 128), f32)],
        cost_estimate=pl.CostEstimate(flops=20 * ROWS * 128, bytes_accessed=4 * ROWS * 512, transcendentals=0),
        name="final_step",
    )(partial, left, right, below, above, velocity, weights)


def body(
    density,
    velocity,
    shear_rates,
    hermite_matrix,
    laguerre_matrix,
    flow_first,
    flow_second,
    stress_weights,
):
    rows = density.reshape(ROWS, 128)
    speeds = velocity.reshape(8, 128)
    shear = shear_rates.reshape(16, 128)
    first = jnp.transpose(flow_first, (1, 0, 2)).reshape(40, 10)
    second = jnp.transpose(flow_second, (1, 0, 2)).reshape(40, 10)
    weights = jnp.transpose(stress_weights.reshape(3, 5, MODES_P), (1, 2, 0))
    place = (lax.axis_index("col") * 5).astype(jnp.int32).reshape(1)

    count_x = lax.axis_size("gx")
    count_y = lax.axis_size("gy")
    ring = [(i, (i + 1) % count_x) for i in range(count_x)]
    back = [(target, source) for source, target in ring]
    line = [(i, i + 1) for i in range(count_y - 1)]
    line_back = [(target, source) for source, target in line]

    low, high = x_halos(rows)
    left = lax.ppermute(high, "gx", ring)
    right = lax.ppermute(low, "gx", back)
    edge_low, edge_high = y_edges(rows)
    below = lax.ppermute(edge_high, "gy", line)
    above = lax.ppermute(edge_low, "gy", line_back)
    other = lax.ppermute(rows, "col", [(0, 1), (1, 0)])
    partial = main(place, laguerre_matrix, rows, other, speeds, shear, first, second, hermite_matrix)
    advanced, stress = final(partial, left, right, below, above, speeds, weights)
    stress = lax.psum(stress, "col")
    return (advanced.reshape(density.shape), stress.reshape(3, 4, 128))


def solution(mesh):
    in_specs = (
        P("col", None, None, "gx", "gy"),
        P(None, "gx", "gy"),
        P(None, "gx", "gy"),
        P(),
        P(),
        P(),
        P(),
        P(None, "col", None, None),
    )
    out_specs = (P("col", None, None, "gx", "gy"), P(None, "gx", "gy"))
    return jax.shard_map(body, mesh=mesh, in_specs=in_specs, out_specs=out_specs, check_vma=False)
```

profile of v0, /device:TPU:257, one launch (start us, length us, event | category | flops | bytes accessed | tf_op | source)
XLA Modules:
  0.0 56.4 jit_solution(11533214671209807823)
XLA Ops:
  0.6 2.6 %collective-permute-start = (f32[2000,128]{1,0:T(8,128)}, f32[2000,128]{1,0:T(8,128)S(1)}, u32[]{:S(2)}, u32[]{:S(2)}) collective-permute-start(f32[2000,128]{1,0:T(8,128)} %bitcast.14), channel_id=1, source_target_pairs={{0,1},{1,0},{2,3},{3,2},{4,5},{5,4},{6,7},{7,6},{8,9},{9,8},{10,11... | collective-permute-start | bytes 3072008 | tf_op jit(solution)/shard_map/ppermute | solution.py:396
  3.2 0.0 copy-start.10
  3.2 3.9 %x_halos.1 = (f32[5,2,104,128]{3,2,1,0:T(8,128)}, f32[5,2,104,128]{3,2,1,0:T(8,128)}) custom-call(f32[2000,128]{1,0:T(8,128)} %bitcast.15), custom_call_target="tpu_custom_call" | custom-call | bytes 2048000 | tf_op jit(solution)/shard_map/x_halos/pallas_call | solution.py:57
  7.1 3.2 %collective-permute-start.1 = (f32[5,2,104,128]{3,2,1,0:T(8,128)}, f32[5,2,104,128]{3,2,1,0:T(8,128)S(1)}, u32[]{:S(2)}, u32[]{:S(2)}) collective-permute-start(f32[5,2,104,128]{3,2,1,0:T(8,128)} %get-tuple-element.8), channel_id=1, source_target_pairs={{0,32},{32,64},{64,96},{96,128},{128,160},{160,192},{192,224},{224... | collective-permute-start | bytes 1597448 | tf_op jit(solution)/shard_map/ppermute | solution.py:391
  10.3 6.2 %collective-permute-start.2 = (f32[5,2,104,128]{3,2,1,0:T(8,128)}, f32[5,2,104,128]{3,2,1,0:T(8,128)S(1)}, u32[]{:S(2)}, u32[]{:S(2)}) collective-permute-start(f32[5,2,104,128]{3,2,1,0:T(8,128)} %get-tuple-element.9), channel_id=1, source_target_pairs={{32,0},{64,32},{96,64},{128,96},{160,128},{192,160},{224,192},{256... | collective-permute-start | bytes 1597448 | tf_op jit(solution)/shard_map/ppermute | solution.py:392
  16.6 5.0 %y_edges.1 = (f32[2,2560]{1,0:T(2,128)}, f32[2,2560]{1,0:T(2,128)}) custom-call(f32[2000,128]{1,0:T(8,128)} %bitcast.16), custom_call_target="tpu_custom_call" | custom-call | bytes 1024000 | tf_op jit(solution)/shard_map/y_edges/pallas_call | solution.py:85
  21.6 7.3 %collective-permute-start.3 = (f32[2,2560]{1,0:T(2,128)}, f32[2,2560]{1,0:T(2,128)S(1)}, u32[]{:S(2)}, u32[]{:S(2)}) collective-permute-start(f32[2,2560]{1,0:T(2,128)} %get-tuple-element.10), channel_id=1, source_target_pairs={{0,2},{2,4},{4,6},{6,8},{8,10},{10,12},{12,14},{14,16},{16,18},{18... | collective-permute-start | bytes 61448 | tf_op jit(solution)/shard_map/ppermute | solution.py:394
  28.9 4.0 %collective-permute-start.4 = (f32[2,2560]{1,0:T(2,128)}, f32[2,2560]{1,0:T(2,128)S(1)}, u32[]{:S(2)}, u32[]{:S(2)}) collective-permute-start(f32[2,2560]{1,0:T(2,128)} %get-tuple-element.11), channel_id=1, source_target_pairs={{2,0},{4,2},{6,4},{8,6},{10,8},{12,10},{14,12},{16,14},{18,16},{20... | collective-permute-start | bytes 61448 | tf_op jit(solution)/shard_map/ppermute | solution.py:395
  32.9 0.1 reshape.37
  33.0 0.0 copy-start.3
  33.0 0.0 copy-start.4
  33.0 0.0 copy-start.5
  33.0 0.0 copy-start.6
  33.1 0.0 copy-start.7
  33.1 0.9 %copy.12 = f32[3,5,100]{0,2,1:T(8,128)} copy(f32[3,5,100]{2,0,1:T(4,128)S(1)} %reshape.37) | data formatting | bytes 12000 | tf_op jit(solution)/shard_map/reshape | solution.py:380
  33.9 0.0 collective-permute-done.other_hbm
  34.0 0.0 copy-done
  34.0 0.6 %copy-done.2 = f32[2,4,128]{2,1,0:T(4,128)S(1)} copy-done((f32[2,4,128]{2,1,0:T(4,128)S(1)}, f32[2,4,128]{2,1,0:T(4,128)}, u32[]{:S(2)}) %copy-start.2) | copy-done | bytes 4120
  34.6 9.9 %main_step.1.partial_ref = f32[2000,128]{1,0:T(8,128)S(1)} custom-call(s32[1]{0:T(128)} %bitcast.place_ref, f32[10,10]{1,0:T(8,128)S(1)} %copy-done.5, f32[2000,128]{1,0:T(8,128)S(1)} %bitcast.17, f32[2000,128]{1,0:T(8,128)S(1)} %collective-permute-done.other_hbm, f32[8,128]{1,0:T(8,128)S(1)} %bitcast.19, f32[16,128]{1,0:T(8,128)S(1)} %bitcast.22, ...), custom_call_target="tpu_custom_call" | custom-call | flops 1101004800 | bytes 3072000 | tf_op jit(solution)/shard_map/main_step/pallas_call | solution.py:266
  44.6 1.0 %copy-done.1 = f32[2000,128]{1,0:T(8,128)} copy-done((f32[2000,128]{1,0:T(8,128)}, f32[2000,128]{1,0:T(8,128)S(1)}, u32[]{:S(2)}) %copy-start.1) | copy-done | bytes 1024024
  45.6 0.0 collective-permute-done.3.below_ref
  45.6 0.0 collective-permute-done.4.above_ref
  45.6 0.0 collective-permute-done.1.left_ref
  45.6 0.0 collective-permute-done.2.right_ref
  45.6 0.0 copy-start.9
  45.6 0.5 copy-done.11
  46.2 0.0 copy-done.12
  46.2 0.2 copy-done.8
  46.4 0.2 copy-done.9
  46.6 5.4 %final_step.1 = (f32[2000,128]{1,0:T(8,128)}, f32[12,128]{1,0:T(8,128)}) custom-call(f32[2000,128]{1,0:T(8,128)} %copy-done.1, f32[5,2,104,128]{3,2,1,0:T(8,128)} %copy-done.8, f32[5,2,104,128]{3,2,1,0:T(8,128)} %copy-done.9, f32[2,2560]{1,0:T(2,128)} %copy-done.11, f32[2,2560]{1,0:T(2,128)} %copy-done.12, f32[8,128]{1,0:T(8,128)} %bitcast.18, ...), custom_call_target="tpu_custom_call" | custom-call | flops 5120000 | bytes 4096000 | tf_op jit(solution)/shard_map/final_step/pallas_call | solution.py:346
  52.0 0.7 %reshape.39 = f32[3,4,128]{2,1,0:T(4,128)S(1)} reshape(f32[12,128]{1,0:T(8,128)} %get-tuple-element.13) | data formatting | bytes 12288 | tf_op jit(solution)/shard_map/reshape | solution.py:400
  52.7 3.7 %psum.7 = f32[3,4,128]{2,1,0:T(4,128)} all-reduce(f32[3,4,128]{2,1,0:T(4,128)S(1)} %reshape.39), channel_id=1, replica_groups=mesh['gx'=16,'gy'=16,'col'=2] {'col'}, use_global_device_ids=true, to_apply=%region_0.0 | all-reduce | flops 1536 | bytes 12288 | tf_op jit(solution)/shard_map/psum | solution.py:399
  (13 shorter events, 0.0 us)
Async XLA Ops:
  0.6 33.3 %collective-permute-start = (f32[2000,128]{1,0:T(8,128)}, f32[2000,128]{1,0:T(8,128)S(1)}, u32[]{:S(2)}, u32[]{:S(2)}) collective-permute-start(f32[2000,128]{1,0:T(8,128)} %bitcast.14), channel_id=1, source_target_pairs={{0,1},{1,0},{2,3},{3,2},{4,5},{5,4},{6,7},{7,6},{8,9},{9,8},{10,11... | collective-permute-start | bytes 3072008 | tf_op jit(solution)/shard_map/ppermute | solution.py:396
  3.2 29.7 %copy-start.10 = (f32[3,5,10,10]{3,0,2,1:T(4,128)S(1)}, f32[3,5,10,10]{3,0,2,1:T(4,128)}, u32[]{:S(2)}) copy-start(f32[3,5,10,10]{3,0,2,1:T(4,128)} %param.15) | copy-start | bytes 18004
  7.1 26.9 %copy-start = (f32[5,10,10,4,128]{4,3,2,1,0:T(4,128)S(1)}, f32[5,10,10,4,128]{4,3,2,1,0:T(4,128)}, u32[]{:S(2)}) copy-start(f32[5,10,10,4,128]{4,3,2,1,0:T(4,128)} %param.8) | copy-start | bytes 3072004
  7.1 38.5 %collective-permute-start.1 = (f32[5,2,104,128]{3,2,1,0:T(8,128)}, f32[5,2,104,128]{3,2,1,0:T(8,128)S(1)}, u32[]{:S(2)}, u32[]{:S(2)}) collective-permute-start(f32[5,2,104,128]{3,2,1,0:T(8,128)} %get-tuple-element.8), channel_id=1, source_target_pairs={{0,32},{32,64},{64,96},{96,128},{128,160},{160,192},{192,224},{224... | collective-permute-start | bytes 1597448 | tf_op jit(solution)/shard_map/ppermute | solution.py:391
  10.3 35.3 %collective-permute-start.2 = (f32[5,2,104,128]{3,2,1,0:T(8,128)}, f32[5,2,104,128]{3,2,1,0:T(8,128)S(1)}, u32[]{:S(2)}, u32[]{:S(2)}) collective-permute-start(f32[5,2,104,128]{3,2,1,0:T(8,128)} %get-tuple-element.9), channel_id=1, source_target_pairs={{32,0},{64,32},{96,64},{128,96},{160,128},{192,160},{224,192},{256... | collective-permute-start | bytes 1597448 | tf_op jit(solution)/shard_map/ppermute | solution.py:392
  21.6 24.0 %collective-permute-start.3 = (f32[2,2560]{1,0:T(2,128)}, f32[2,2560]{1,0:T(2,128)S(1)}, u32[]{:S(2)}, u32[]{:S(2)}) collective-permute-start(f32[2,2560]{1,0:T(2,128)} %get-tuple-element.10), channel_id=1, source_target_pairs={{0,2},{2,4},{4,6},{6,8},{8,10},{10,12},{12,14},{14,16},{16,18},{18... | collective-permute-start | bytes 61448 | tf_op jit(solution)/shard_map/ppermute | solution.py:394
  28.9 16.7 %collective-permute-start.4 = (f32[2,2560]{1,0:T(2,128)}, f32[2,2560]{1,0:T(2,128)S(1)}, u32[]{:S(2)}, u32[]{:S(2)}) collective-permute-start(f32[2,2560]{1,0:T(2,128)} %get-tuple-element.11), channel_id=1, source_target_pairs={{2,0},{4,2},{6,4},{8,6},{10,8},{12,10},{14,12},{16,14},{18,16},{20... | collective-permute-start | bytes 61448 | tf_op jit(solution)/shard_map/ppermute | solution.py:395
  33.0 0.9 %copy-start.3 = (f32[4,10,10]{2,0,1:T(4,128)S(1)}, f32[4,10,10]{2,0,1:T(4,128)}, u32[]{:S(2)}) copy-start(f32[4,10,10]{2,0,1:T(4,128)} %param.13) | copy-start | bytes 4804
  33.0 0.9 %copy-start.4 = (f32[4,10,10]{2,0,1:T(4,128)S(1)}, f32[4,10,10]{2,0,1:T(4,128)}, u32[]{:S(2)}) copy-start(f32[4,10,10]{2,0,1:T(4,128)} %param.14) | copy-start | bytes 4804
  33.0 0.9 %copy-start.5 = (f32[10,10]{1,0:T(8,128)S(1)}, f32[10,10]{1,0:T(8,128)}, u32[]{:S(2)}) copy-start(f32[10,10]{1,0:T(8,128)} %laguerre_ref.1) | copy-start | bytes 1204
  33.0 0.9 %copy-start.6 = (f32[4,4,128]{2,1,0:T(4,128)S(1)}, f32[4,4,128]{2,1,0:T(4,128)}, u32[]{:S(2)}) copy-start(f32[4,4,128]{2,1,0:T(4,128)} %param.10) | copy-start | bytes 24580
  33.1 0.9 %copy-start.7 = (f32[10,10]{1,0:T(8,128)S(1)}, f32[10,10]{1,0:T(8,128)}, u32[]{:S(2)}) copy-start(f32[10,10]{1,0:T(8,128)} %hermite_ref.1) | copy-start | bytes 1204
  33.9 0.7 %copy-start.2 = (f32[2,4,128]{2,1,0:T(4,128)S(1)}, f32[2,4,128]{2,1,0:T(4,128)}, u32[]{:S(2)}) copy-start(f32[2,4,128]{2,1,0:T(4,128)} %param.9) | copy-start | bytes 12292
  44.6 1.0 %copy-start.1 = (f32[2000,128]{1,0:T(8,128)}, f32[2000,128]{1,0:T(8,128)S(1)}, u32[]{:S(2)}) copy-start(f32[2000,128]{1,0:T(8,128)S(1)} %main_step.1.partial_ref) | copy-start | bytes 3072004
  45.6 0.6 %copy-start.11 = (f32[2,2560]{1,0:T(2,128)}, f32[2,2560]{1,0:T(2,128)S(1)}, u32[]{:S(2)}) copy-start(f32[2,2560]{1,0:T(2,128)S(1)} %collective-permute-done.3.below_ref) | copy-start | bytes 61444
  45.6 0.6 %copy-start.12 = (f32[2,2560]{1,0:T(2,128)}, f32[2,2560]{1,0:T(2,128)S(1)}, u32[]{:S(2)}) copy-start(f32[2,2560]{1,0:T(2,128)S(1)} %collective-permute-done.4.above_ref) | copy-start | bytes 61444
  45.6 0.8 %copy-start.8 = (f32[5,2,104,128]{3,2,1,0:T(8,128)}, f32[5,2,104,128]{3,2,1,0:T(8,128)S(1)}, u32[]{:S(2)}) copy-start(f32[5,2,104,128]{3,2,1,0:T(8,128)S(1)} %collective-permute-done.1.left_ref) | copy-start | bytes 1597444
  45.6 1.0 %copy-start.9 = (f32[5,2,104,128]{3,2,1,0:T(8,128)}, f32[5,2,104,128]{3,2,1,0:T(8,128)S(1)}, u32[]{:S(2)}) copy-start(f32[5,2,104,128]{3,2,1,0:T(8,128)S(1)} %collective-permute-done.2.right_ref) | copy-start | bytes 1597444
where the time goes:
time: 56.9 us; the launch traced here: 56.4 us
  Pallas kernels  24.2 us (43%)
  starting transfers between devices  23.3 us (41%)
  local copies, waits for them, and re-layouts  4.32 us (8%)
  blocking collectives  3.69 us (6%)
  between operations  0.84 us (1%)
    pallas_call x1, Pallas kernels, main(): pl.pallas_call(main_kernel, in_specs=[smem, smem, hbm, hbm, vmem, vmem, v...  9.94 us
    ppermute x1, starting transfers between devices, body(): below = lax.ppermute(edge_high, 'gy', line)  7.29 us
    ppermute x1, starting transfers between devices, body(): right = lax.ppermute(low, 'gx', back)  6.23 us
    pallas_call x1, Pallas kernels, final(): pl.pallas_call(final_kernel, grid=(5,), in_specs=[rows, halo, halo, edge,...  5.36 us
    pallas_call x1, Pallas kernels, y_edges(): pl.pallas_call(edge_kernel, grid=(5,), in_specs=[pl.BlockSpec((400, 128),...  5.01 us
    ppermute x1, starting transfers between devices, body(): above = lax.ppermute(edge_low, 'gy', line_back)  4 us
    pallas_call x1, Pallas kernels, x_halos(): pl.pallas_call(halo_kernel, grid=(5,), in_specs=[pl.BlockSpec((400, 128),...  3.85 us
    psum x1, blocking collectives, body(): stress = lax.psum(stress, 'col')  3.69 us
  transfers between devices with their start and end apart: 5, of which 0 were waited for; matrix products, arithmetic and copies ran while one was open for 2% of the time, Pallas kernels for 33%

commit v1 on v0

--- a/solution.py
+++ b/solution.py
@@ -22,6 +22,11 @@
 MODES_PAD = 104
 
 
+vmem = pl.BlockSpec(memory_space=pltpu.VMEM)
+smem = pl.BlockSpec(memory_space=pltpu.SMEM)
+hbm = pl.BlockSpec(memory_space=pl.ANY)
+
+
 def upwind(speed):
     plus = jnp.maximum(speed, 0.0)
     minus = jnp.minimum(speed, 0.0)
@@ -46,50 +51,51 @@
 
 
 def halo_kernel(x_ref, low_ref, high_ref):
-    for k in range(2):
-        low_ref[0, k, 0:MODES_P, :] = x_ref[pl.ds(k, MODES_P, stride=4), :]
-        high_ref[0, k, 0:MODES_P, :] = x_ref[pl.ds(2 + k, MODES_P, stride=4), :]
+    for p in range(5):
+        for k in range(2):
+            low_ref[p, k, 0:MODES_P, :] = x_ref[pl.ds(400 * p + k, MODES_P, stride=4), :]
+            high_ref[p, k, 0:MODES_P, :] = x_ref[pl.ds(400 * p + 2 + k, MODES_P, stride=4), :]
 
 
 def x_halos(rows):
     shape = jax.ShapeDtypeStruct((5, 2, MODES_PAD, 128), f32)
-    spec = pl.BlockSpec((1, 2, MODES_PAD, 128), lambda p: (p, 0, 0, 0))
     return pl.pallas_call(
         halo_kernel,
-        grid=(5,),
-        in_specs=[pl.BlockSpec((400, 128), lambda p: (p, 0))],
-        out_specs=[spec, spec],
+        in_specs=[vmem],
+        out_specs=[vmem, vmem],
         out_shape=[shape, shape],
         cost_estimate=pl.CostEstimate(flops=0, bytes_accessed=2 * ROWS * 512, transcendentals=0),
+        compiler_params=pltpu.CompilerParams(vmem_limit_bytes=16 << 20),
         name="x_halos",
     )(rows)
 
 
 def edge_kernel(x_ref, low_ref, high_ref, rows_ref):
-    rows_ref[96:128, :] = jnp.zeros((32, 128), f32)
-    lane = iota((8, 128), 1)
-    row = iota((8, 128), 0)
-    pick = one_hot(((row < 2) & (lane == row)) | ((row >= 2) & (row < 4) & (lane == row + 124)))
     for x in range(4):
-        rows_ref[0:MODES_P, :] = x_ref[pl.ds(x, MODES_P, stride=4), :]
-        edges = lax.dot_general(
-            pick, rows_ref[...], (((1,), (1,)), ((), ())), precision=highest, preferred_element_type=f32
-        )
-        low_ref[:, x * 128 : (x + 1) * 128] = edges[0:2]
-        high_ref[:, x * 128 : (x + 1) * 128] = edges[2:4]
+        rows_ref[x * 128 + 96 : (x + 1) * 128, :] = jnp.zeros((32, 256), bf16)
+    lane = lax.rem(iota((8, 256), 1), 128)
+    row = iota((8, 256), 0)
+    pick = one_hot(((row < 2) & (lane == row)) | ((row >= 2) & (row < 4) & (lane == row + 124))).astype(bf16)
+    for p in range(5):
+        for x in range(4):
+            high, low = split(x_ref[pl.ds(400 * p + x, MODES_P, stride=4), :])
+            rows_ref[x * 128 : x * 128 + MODES_P, 0:128] = high
+            rows_ref[x * 128 : x * 128 + MODES_P, 128:256] = low
+        edges = lax.dot_general(pick, rows_ref[...], (((1,), (1,)), ((), ())), preferred_element_type=f32)
+        low_ref[:, p * 512 : (p + 1) * 512] = edges[0:2]
+        high_ref[:, p * 512 : (p + 1) * 512] = edges[2:4]
 
 
 def y_edges(rows):
     shape = jax.ShapeDtypeStruct((2, 5 * 512), f32)
-    spec = pl.BlockSpec((2, 512), lambda p: (0, p))
     return pl.pallas_call(
         edge_kernel,
-        grid=(5,),
-        in_specs=[pl.BlockSpec((400, 128), lambda p: (p, 0))],
-        out_specs=[spec, spec],
+        in_specs=[vmem],
+        out_specs=[vmem, vmem],
         out_shape=[shape, shape],
-        scratch_shapes=[pltpu.VMEM((128, 128), f32)],
+        scratch_shapes=[pltpu.VMEM((512, 256), bf16)],
         cost_estimate=pl.CostEstimate(flops=0, bytes_accessed=ROWS * 512, transcendentals=0),
+        compiler_params=pltpu.CompilerParams(vmem_limit_bytes=16 << 20),
         name="y_edges",
     )(rows)
 
@@ -157,7 +163,7 @@
     first_ref,
     second_ref,
     hermite_ref,
-    out_hbm,
+    out_ref,
     own_ref,
     other_ref,
     turned_ref,
@@ -254,19 +260,16 @@
         return carry
 
     lax.fori_loop(0, PQ_PAD // 8, strip, 0)
-    copy_out = pltpu.make_async_copy(result_ref.at[0:ROWS], out_hbm, sems.at[2])
+    copy_out = pltpu.make_async_copy(result_ref.at[0:ROWS], out_ref, sems.at[2])
     copy_out.start()
     copy_out.wait()
 
 
 def main(place, laguerre, own, other, velocity, shear, first, second, hermite):
-    vmem = pl.BlockSpec(memory_space=pltpu.VMEM)
-    smem = pl.BlockSpec(memory_space=pltpu.SMEM)
-    hbm = pl.BlockSpec(memory_space=pl.ANY)
     return pl.pallas_call(
         main_kernel,
         in_specs=[smem, smem, hbm, hbm, vmem, vmem, vmem, vmem, vmem],
-        out_specs=hbm,
+        out_specs=vmem,
         out_shape=jax.ShapeDtypeStruct((ROWS, 128), f32),
         scratch_shapes=[
             pltpu.VMEM((K_HALF * RX, 128), f32),
@@ -286,9 +289,8 @@
 
 
 def final_kernel(
-    partial_ref, left_ref, right_ref, below_ref, above_ref, velocity_ref, weight_ref, out_ref, stress_ref
+    partial_ref, left_ref, right_ref, below_ref, above_ref, velocity_ref, weight_ref, out_hbm, stress_ref, out_ref, sems
 ):
-    p = pl.program_id(0)
     u = velocity_ref[0:4, :]
     v = velocity_ref[4:8, :]
     lane4 = iota((4, 128), 1)
@@ -296,68 +298,63 @@
     _, vm1, vm2, vp1, vp2 = upwind(v)
     near = jnp.where(lane4 == 0, vm1, jnp.where(lane4 == 127, vp1, 0.0))
     far = jnp.where(lane4 <= 1, vm2, jnp.where(lane4 >= 126, vp2, 0.0))
-
-    edges = jnp.concatenate([below_ref[...], above_ref[...], jnp.zeros((4, 512), f32)], axis=0)
-    high = edges.astype(bf16).astype(f32)
-    rest = edges - high
-    middle = rest.astype(bf16).astype(f32)
-    low = rest - middle
-    stacked = jnp.concatenate([high, middle, low, jnp.zeros((8, 512), f32)], axis=0).astype(bf16)
     row = lax.rem(iota((32, 256), 0), 8)
     lane = iota((32, 256), 1)
     hit = (row == 1) & ((lane == 0) | (lane == 129))
     hit = hit | ((row == 2) & ((lane == 127) | (lane == 254)))
     hit = hit | ((row == 0) & (lane == 128))
     hit = hit | ((row == 3) & (lane == 255))
-    spread = lax.dot_general(
-        stacked, one_hot(hit).astype(bf16), (((0,), (0,)), ((), ())), preferred_element_type=f32
-    )
-
-    @pl.when(p == 0)
-    def _():
-        stress_ref[...] = jnp.zeros_like(stress_ref)
-
-    left_far = left_ref[0, 0, 0:MODES_P, :]
-    left_near = left_ref[0, 1, 0:MODES_P, :]
-    right_near = right_ref[0, 0, 0:MODES_P, :]
-    right_far = right_ref[0, 1, 0:MODES_P, :]
-    for x in range(4):
-        total = partial_ref[pl.ds(x, MODES_P, stride=4), :]
-        total = total + near[x : x + 1] * spread[x * 128 : x * 128 + MODES_P, 0:128]
-        total = total + far[x : x + 1] * spread[x * 128 : x * 128 + MODES_P, 128:256]
-        if x == 0:
-            total = total + um1[0:1] * left_near + um2[0:1] * left_far
-        if x == 1:
-            total = total + um2[1:2] * left_near
-        if x == 2:
-            total = total + up2[2:3] * right_near
-        if x == 3:
-            total = total + up1[3:4] * right_near + up2[3:4] * right_far
-        out_ref[pl.ds(x, MODES_P, stride=4), :] = total
-        for s in range(3):
-            moment = jnp.sum(weight_ref[0, :, s : s + 1] * total, axis=0, keepdims=True)
-            stress_ref[4 * s + x : 4 * s + x + 1, :] += moment
+    place = one_hot(hit).astype(bf16)
+    stress = [jnp.zeros((1, 128), f32) for _ in range(12)]
+    copies = []
+    for p in range(5):
+        lanes = slice(p * 512, (p + 1) * 512)
+        edges = jnp.concatenate([below_ref[:, lanes], above_ref[:, lanes], jnp.zeros((4, 512), f32)], axis=0)
+        high = edges.astype(bf16).astype(f32)
+        rest = edges - high
+        middle = rest.astype(bf16).astype(f32)
+        low = rest - middle
+        stacked = jnp.concatenate([high, middle, low, jnp.zeros((8, 512), f32)], axis=0).astype(bf16)
+        spread = lax.dot_general(stacked, place, (((0,), (0,)), ((), ())), preferred_element_type=f32)
+        left_far = left_ref[p, 0, 0:MODES_P, :]
+        left_near = left_ref[p, 1, 0:MODES_P, :]
+        right_near = right_ref[p, 0, 0:MODES_P, :]
+        right_far = right_ref[p, 1, 0:MODES_P, :]
+        for x in range(4):
+            total = partial_ref[pl.ds(400 * p + x, MODES_P, stride=4), :]
+            total = total + near[x : x + 1] * spread[x * 128 : x * 128 + MODES_P, 0:128]
+            total = total + far[x : x + 1] * spread[x * 128 : x * 128 + MODES_P, 128:256]
+            if x == 0:
+                total = total + um1[0:1] * left_near + um2[0:1] * left_far
+            if x == 1:
+                total = total + um2[1:2] * left_near
+            if x == 2:
+                total = total + up2[2:3] * right_near
+            if x == 3:
+                total = total + up1[3:4] * right_near + up2[3:4] * right_far
+            out_ref[pl.ds(400 * p + x, MODES_P, stride=4), :] = total
+            for s in range(3):
+                moment = jnp.sum(weight_ref[p, :, s : s + 1] * total, axis=0, keepdims=True)
+                stress[4 * s + x] = stress[4 * s + x] + moment
+        rows = pl.ds(400 * p, 400)
+        copies.append(pltpu.make_async_copy(out_ref.at[rows], out_hbm.at[rows], sems.at[p]))
+        copies[-1].start()
+    for s in range(3):
+        for x in range(4):
+            stress_ref[s, x : x + 1, :] = stress[4 * s + x]
+    for copy in copies:
+        copy.wait()
 
 
 def final(partial, left, right, below, above, velocity, weights):
-    halo = pl.BlockSpec((1, 2, MODES_PAD, 128), lambda p: (p, 0, 0, 0))
-    edge = pl.BlockSpec((2, 512), lambda p: (0, p))
-    rows = pl.BlockSpec((400, 128), lambda p: (p, 0))
     return pl.pallas_call(
         final_kernel,
-        grid=(5,),
-        in_specs=[
-            rows,
-            halo,
-            halo,
-            edge,
-            edge,
-            pl.BlockSpec((8, 128), lambda p: (0, 0)),
-            pl.BlockSpec((1, MODES_P, 3), lambda p: (p, 0, 0)),
-        ],
-        out_specs=[rows, pl.BlockSpec((12, 128), lambda p: (0, 0))],
-        out_shape=[jax.ShapeDtypeStruct((ROWS, 128), f32), jax.ShapeDtypeStruct((12, 128), f32)],
+        in_specs=[vmem] * 7,
+        out_specs=[hbm, vmem],
+        out_shape=[jax.ShapeDtypeStruct((ROWS, 128), f32), jax.ShapeDtypeStruct((3, 4, 128), f32)],
+        scratch_shapes=[pltpu.VMEM((ROWS, 128), f32), pltpu.SemaphoreType.DMA((5,))],
         cost_estimate=pl.CostEstimate(flops=20 * ROWS * 128, bytes_accessed=4 * ROWS * 512, transcendentals=0),
+        compiler_params=pltpu.CompilerParams(vmem_limit_bytes=16 << 20),
         name="final_step",
     )(partial, left, right, below, above, velocity, weights)
 
@@ -397,7 +394,7 @@
     partial = main(place, laguerre_matrix, rows, other, speeds, shear, first, second, hermite_matrix)
     advanced, stress = final(partial, left, right, below, above, speeds, weights)
     stress = lax.psum(stress, "col")
-    return (advanced.reshape(density.shape), stress.reshape(3, 4, 128))
+    return (advanced.reshape(density.shape), stress)
 
 
 def solution(mesh):

time: 56.9 us -> 43.4 us (0.76)
  Pallas kernels: 24.2 us -> 12.9 us
  local copies, waits for them, and re-layouts: 4.32 us -> 2.2 us
    pallas_call x3, Pallas kernels: 14.2 us -> 2.99 us  [the longest x1 1.46 us: final(): pl.pallas_call(final_kernel, in_specs=[vmem] * 7, out_specs=[hbm, vmem],...]
    unnamed x27 -> x19, local copies, waits for them, and re-layouts: 2.64 us -> 1.93 us
    reshape x1 -> x0, local copies, waits for them, and re-layouts: 0.7 us -> none  [body(): return (advanced.reshape(density.shape), stress.reshape(3, 4, 128))]
    reshape x2, local copies, waits for them, and re-layouts: 0.97 us -> 0.27 us  [body(): weights = jnp.transpose(stress_weights.reshape(3, 5, MODES_P), (1, 2, 0))]
  transfers between devices with their start and end apart: 5 -> 5, of which waited for: 0 -> 0; matrix products, arithmetic and copies ran while one was open for 2% -> 1% of each run, Pallas kernels for 33% -> 27%
where the time goes in v1:
time: 43.4 us; the launch traced here: 43 us
  starting transfers between devices  23.4 us (54%)
  Pallas kernels  12.9 us (30%)
  blocking collectives  3.73 us (9%)
  local copies, waits for them, and re-layouts  2.2 us (5%)
  between operations  0.82 us (2%)
    pallas_call x1, Pallas kernels, main(): pl.pallas_call(main_kernel, in_specs=[smem, smem, hbm, hbm, vmem, vmem, v...  9.93 us
    ppermute x1, starting transfers between devices, body(): below = lax.ppermute(edge_high, 'gy', line)  7.31 us
    ppermute x1, starting transfers between devices, body(): right = lax.ppermute(low, 'gx', back)  6.23 us
    ppermute x1, starting transfers between devices, body(): above = lax.ppermute(edge_low, 'gy', line_back)  4 us
    psum x1, blocking collectives, body(): stress = lax.psum(stress, 'col')  3.73 us
    ppermute x1, starting transfers between devices, body(): left = lax.ppermute(high, 'gx', ring)  3.24 us
    ppermute x1, starting transfers between devices, body(): other = lax.ppermute(rows, 'col', [(0, 1), (1, 0)])  2.59 us
    unnamed x19, local copies, waits for them, and re-layouts  1.93 us
  transfers between devices with their start and end apart: 5, of which 0 were waited for; matrix products, arithmetic and copies ran while one was open for 1% of the time, Pallas kernels for 27%

profile of v1, /device:TPU:257, one launch (start us, length us, event | category | flops | bytes accessed | tf_op | source)
XLA Modules:
  0.0 43.0 jit_solution(8012286071363397412)
XLA Ops:
  0.6 2.6 %collective-permute-start = (f32[2000,128]{1,0:T(8,128)}, f32[2000,128]{1,0:T(8,128)S(1)}, u32[]{:S(2)}, u32[]{:S(2)}) collective-permute-start(f32[2000,128]{1,0:T(8,128)} %bitcast.14), channel_id=1, source_target_pairs={{0,1},{1,0},{2,3},{3,2},{4,5},{5,4},{6,7},{7,6},{8,9},{9,8},{10,11... | collective-permute-start | bytes 3072008 | tf_op jit(solution)/shard_map/ppermute | solution.py:393
  3.2 0.0 copy-start
  3.2 1.2 %copy-done = f32[5,10,10,4,128]{4,3,2,1,0:T(4,128)S(1)} copy-done((f32[5,10,10,4,128]{4,3,2,1,0:T(4,128)S(1)}, f32[5,10,10,4,128]{4,3,2,1,0:T(4,128)}, u32[]{:S(2)}) %copy-start) | copy-done | bytes 1024024
  4.4 1.0 %x_halos.1 = (f32[5,2,104,128]{3,2,1,0:T(8,128)}, f32[5,2,104,128]{3,2,1,0:T(8,128)}) custom-call(f32[2000,128]{1,0:T(8,128)S(1)} %bitcast.15), custom_call_target="tpu_custom_call" | custom-call | bytes 2048000 | tf_op jit(solution)/shard_map/x_halos/pallas_call | solution.py:62
  5.5 3.2 %collective-permute-start.1 = (f32[5,2,104,128]{3,2,1,0:T(8,128)}, f32[5,2,104,128]{3,2,1,0:T(8,128)S(1)}, u32[]{:S(2)}, u32[]{:S(2)}) collective-permute-start(f32[5,2,104,128]{3,2,1,0:T(8,128)} %get-tuple-element.8), channel_id=1, source_target_pairs={{0,32},{32,64},{64,96},{96,128},{128,160},{160,192},{192,224},{224... | collective-permute-start | bytes 1597448 | tf_op jit(solution)/shard_map/ppermute | solution.py:388
  8.7 6.2 %collective-permute-start.2 = (f32[5,2,104,128]{3,2,1,0:T(8,128)}, f32[5,2,104,128]{3,2,1,0:T(8,128)S(1)}, u32[]{:S(2)}, u32[]{:S(2)}) collective-permute-start(f32[5,2,104,128]{3,2,1,0:T(8,128)} %get-tuple-element.9), channel_id=1, source_target_pairs={{32,0},{64,32},{96,64},{128,96},{160,128},{192,160},{224,192},{256... | collective-permute-start | bytes 1597448 | tf_op jit(solution)/shard_map/ppermute | solution.py:389
  15.0 0.5 %y_edges.1 = (f32[2,2560]{1,0:T(2,128)S(1)}, f32[2,2560]{1,0:T(2,128)S(1)}) custom-call(f32[2000,128]{1,0:T(8,128)S(1)} %bitcast.16), custom_call_target="tpu_custom_call" | custom-call | bytes 1024000 | tf_op jit(solution)/shard_map/y_edges/pallas_call | solution.py:91
  15.5 7.3 %collective-permute-start.3 = (f32[2,2560]{1,0:T(2,128)S(1)}, f32[2,2560]{1,0:T(2,128)S(1)}, u32[]{:S(2)}, u32[]{:S(2)}) collective-permute-start(f32[2,2560]{1,0:T(2,128)S(1)} %get-tuple-element.10), channel_id=1, source_target_pairs={{0,2},{2,4},{4,6},{6,8},{8,10},{10,12},{12,14},{14,16},{16,18},{18... | collective-permute-start | bytes 61448 | tf_op jit(solution)/shard_map/ppermute | solution.py:391
  22.8 4.0 %collective-permute-start.4 = (f32[2,2560]{1,0:T(2,128)S(1)}, f32[2,2560]{1,0:T(2,128)S(1)}, u32[]{:S(2)}, u32[]{:S(2)}) collective-permute-start(f32[2,2560]{1,0:T(2,128)S(1)} %get-tuple-element.11), channel_id=1, source_target_pairs={{2,0},{4,2},{6,4},{8,6},{10,8},{12,10},{14,12},{16,14},{18,16},{20... | collective-permute-start | bytes 61448 | tf_op jit(solution)/shard_map/ppermute | solution.py:392
  26.8 0.0 copy-done.8
  26.8 0.1 reshape.34
  26.9 0.0 copy-start.3
  26.9 0.0 copy-start.4
  26.9 0.0 copy-start.5
  27.0 0.0 copy-start.6
  27.0 0.0 copy-start.7
  27.0 0.2 copy.12
  27.2 0.0 collective-permute-done.other_hbm
  27.2 0.0 copy-start.2
  27.2 0.0 copy-done.1
  27.2 0.5 %copy-done.3 = f32[4,10,10]{2,0,1:T(4,128)S(1)} copy-done((f32[4,10,10]{2,0,1:T(4,128)S(1)}, f32[4,10,10]{2,0,1:T(4,128)}, u32[]{:S(2)}) %copy-start.3) | copy-done | bytes 1624
  27.6 0.0 copy-done.4
  27.7 0.0 copy-done.5
  27.7 0.0 copy-done.7
  27.7 0.2 copy-done.2
  27.9 9.9 %main_step.1.partial_ref = f32[2000,128]{1,0:T(8,128)S(1)} custom-call(s32[1]{0:T(128)} %bitcast.place_ref, f32[10,10]{1,0:T(8,128)S(1)} %copy-done.5, f32[2000,128]{1,0:T(8,128)S(1)} %bitcast.17, f32[2000,128]{1,0:T(8,128)S(1)} %collective-permute-done.other_hbm, f32[8,128]{1,0:T(8,128)S(1)} %bitcast.19, f32[16,128]{1,0:T(8,128)S(1)} %bitcast.23, ...), custom_call_target="tpu_custom_call" | custom-call | flops 1101004800 | bytes 3072000 | tf_op jit(solution)/shard_map/main_step/pallas_call | solution.py:269
  37.8 0.0 collective-permute-done.3.below_ref
  37.8 0.0 collective-permute-done.4.above_ref
  37.8 0.0 collective-permute-done.1.left_ref
  37.8 0.0 collective-permute-done.2.right_ref
  37.8 1.5 %final_step.1 = (f32[2000,128]{1,0:T(8,128)}, f32[3,4,128]{2,1,0:T(4,128)S(1)}) custom-call(f32[2000,128]{1,0:T(8,128)S(1)} %main_step.1.partial_ref, f32[5,2,104,128]{3,2,1,0:T(8,128)S(1)} %collective-permute-done.1.left_ref, f32[5,2,104,128]{3,2,1,0:T(8,128)S(1)} %collective-permute-done.2.right_ref, f32[2,2560]{1,0:T(2,128)S(1)} %collective-permute-done.3.below_ref, ...), custom_call_target="tpu_custom_call" | custom-call | flops 5120000 | bytes 4096000 | tf_op jit(solution)/shard_map/final_step/pallas_call | solution.py:350
  39.3 3.7 %psum.7 = f32[3,4,128]{2,1,0:T(4,128)} all-reduce(f32[3,4,128]{2,1,0:T(4,128)S(1)} %get-tuple-element.13), channel_id=1, replica_groups=mesh['gx'=16,'gy'=16,'col'=2] {'col'}, use_global_device_ids=true, to_apply=%region_0.0 | all-reduce | flops 1536 | bytes 12288 | tf_op jit(solution)/shard_map/psum | solution.py:396
  (4 shorter events, 0.0 us)
Async XLA Ops:
  0.6 26.5 %collective-permute-start = (f32[2000,128]{1,0:T(8,128)}, f32[2000,128]{1,0:T(8,128)S(1)}, u32[]{:S(2)}, u32[]{:S(2)}) collective-permute-start(f32[2000,128]{1,0:T(8,128)} %bitcast.14), channel_id=1, source_target_pairs={{0,1},{1,0},{2,3},{3,2},{4,5},{5,4},{6,7},{7,6},{8,9},{9,8},{10,11... | collective-permute-start | bytes 3072008 | tf_op jit(solution)/shard_map/ppermute | solution.py:393
  3.2 1.2 %copy-start = (f32[5,10,10,4,128]{4,3,2,1,0:T(4,128)S(1)}, f32[5,10,10,4,128]{4,3,2,1,0:T(4,128)}, u32[]{:S(2)}) copy-start(f32[5,10,10,4,128]{4,3,2,1,0:T(4,128)} %param.8) | copy-start | bytes 3072004
  4.4 22.3 %copy-start.8 = (f32[3,5,10,10]{3,0,2,1:T(4,128)S(1)}, f32[3,5,10,10]{3,0,2,1:T(4,128)}, u32[]{:S(2)}) copy-start(f32[3,5,10,10]{3,0,2,1:T(4,128)} %param.15) | copy-start | bytes 18004
  5.5 21.7 %copy-start.1 = (f32[5,10,10,4,128]{4,3,2,1,0:T(4,128)S(1)}, f32[5,10,10,4,128]{4,3,2,1,0:T(4,128)}, u32[]{:S(2)}) copy-start(f32[5,10,10,4,128]{4,3,2,1,0:T(4,128)} %param.8) | copy-start | bytes 3072004
  5.5 32.3 %collective-permute-start.1 = (f32[5,2,104,128]{3,2,1,0:T(8,128)}, f32[5,2,104,128]{3,2,1,0:T(8,128)S(1)}, u32[]{:S(2)}, u32[]{:S(2)}) collective-permute-start(f32[5,2,104,128]{3,2,1,0:T(8,128)} %get-tuple-element.8), channel_id=1, source_target_pairs={{0,32},{32,64},{64,96},{96,128},{128,160},{160,192},{192,224},{224... | collective-permute-start | bytes 1597448 | tf_op jit(solution)/shard_map/ppermute | solution.py:388
  8.7 29.1 %collective-permute-start.2 = (f32[5,2,104,128]{3,2,1,0:T(8,128)}, f32[5,2,104,128]{3,2,1,0:T(8,128)S(1)}, u32[]{:S(2)}, u32[]{:S(2)}) collective-permute-start(f32[5,2,104,128]{3,2,1,0:T(8,128)} %get-tuple-element.9), channel_id=1, source_target_pairs={{32,0},{64,32},{96,64},{128,96},{160,128},{192,160},{224,192},{256... | collective-permute-start | bytes 1597448 | tf_op jit(solution)/shard_map/ppermute | solution.py:389
  15.5 22.4 %collective-permute-start.3 = (f32[2,2560]{1,0:T(2,128)S(1)}, f32[2,2560]{1,0:T(2,128)S(1)}, u32[]{:S(2)}, u32[]{:S(2)}) collective-permute-start(f32[2,2560]{1,0:T(2,128)S(1)} %get-tuple-element.10), channel_id=1, source_target_pairs={{0,2},{2,4},{4,6},{6,8},{8,10},{10,12},{12,14},{14,16},{16,18},{18... | collective-permute-start | bytes 61448 | tf_op jit(solution)/shard_map/ppermute | solution.py:391
  22.8 15.0 %collective-permute-start.4 = (f32[2,2560]{1,0:T(2,128)S(1)}, f32[2,2560]{1,0:T(2,128)S(1)}, u32[]{:S(2)}, u32[]{:S(2)}) collective-permute-start(f32[2,2560]{1,0:T(2,128)S(1)} %get-tuple-element.11), channel_id=1, source_target_pairs={{2,0},{4,2},{6,4},{8,6},{10,8},{12,10},{14,12},{16,14},{18,16},{20... | collective-permute-start | bytes 61448 | tf_op jit(solution)/shard_map/ppermute | solution.py:392
  26.9 0.7 %copy-start.3 = (f32[4,10,10]{2,0,1:T(4,128)S(1)}, f32[4,10,10]{2,0,1:T(4,128)}, u32[]{:S(2)}) copy-start(f32[4,10,10]{2,0,1:T(4,128)} %param.13) | copy-start | bytes 4804
  26.9 0.7 %copy-start.4 = (f32[4,10,10]{2,0,1:T(4,128)S(1)}, f32[4,10,10]{2,0,1:T(4,128)}, u32[]{:S(2)}) copy-start(f32[4,10,10]{2,0,1:T(4,128)} %param.14) | copy-start | bytes 4804
  26.9 0.7 %copy-start.5 = (f32[10,10]{1,0:T(8,128)S(1)}, f32[10,10]{1,0:T(8,128)}, u32[]{:S(2)}) copy-start(f32[10,10]{1,0:T(8,128)} %laguerre_ref.1) | copy-start | bytes 1204
  27.0 0.7 %copy-start.6 = (f32[4,4,128]{2,1,0:T(4,128)S(1)}, f32[4,4,128]{2,1,0:T(4,128)}, u32[]{:S(2)}) copy-start(f32[4,4,128]{2,1,0:T(4,128)} %param.10) | copy-start | bytes 24580
  27.0 0.7 %copy-start.7 = (f32[10,10]{1,0:T(8,128)S(1)}, f32[10,10]{1,0:T(8,128)}, u32[]{:S(2)}) copy-start(f32[10,10]{1,0:T(8,128)} %hermite_ref.1) | copy-start | bytes 1204
  27.2 0.7 %copy-start.2 = (f32[2,4,128]{2,1,0:T(4,128)S(1)}, f32[2,4,128]{2,1,0:T(4,128)}, u32[]{:S(2)}) copy-start(f32[2,4,128]{2,1,0:T(4,128)} %param.9) | copy-start | bytes 12292

commit v2 on v1

--- a/solution.py
+++ b/solution.py
@@ -20,6 +20,9 @@
 N_PAIR = 20
 MODES_P = 100
 MODES_PAD = 104
+PACK_UNROLL = 40
+PAIR_UNROLL = 20
+STRIP_UNROLL = 1
 
 
 vmem = pl.BlockSpec(memory_space=pltpu.VMEM)
@@ -156,32 +159,21 @@
 def main_kernel(
     place_ref,
     laguerre_ref,
-    own_hbm,
-    other_hbm,
+    own_ref,
+    other_ref,
     velocity_ref,
     shear_ref,
     first_ref,
     second_ref,
     hermite_ref,
     out_ref,
-    own_ref,
-    other_ref,
+    data_ref,
     turned_ref,
     rate_ref,
-    result_ref,
     wide_ref,
     narrow_ref,
     coef_ref,
-    sems,
 ):
-    copy_own = pltpu.make_async_copy(own_hbm, own_ref.at[0:ROWS], sems.at[0])
-    copy_other = pltpu.make_async_copy(other_hbm, other_ref.at[0:ROWS], sems.at[1])
-    copy_own.start()
-    copy_other.start()
-    zeros = jnp.zeros((K_HALF * RX - ROWS, 128), f32)
-    own_ref[ROWS:, :] = zeros
-    other_ref[ROWS:, :] = zeros
-
     matrix = coupling(place_ref[0], first_ref[...], second_ref[...], hermite_ref[...])
     matrix_high, matrix_low = split(matrix)
     wide_ref[:, 0:128] = matrix_high
@@ -207,20 +199,24 @@
     for i, c in enumerate(coefs):
         coef_ref[i, 0:4, :] = c
 
-    copy_own.wait()
-    copy_other.wait()
+    def pack(rx, carry):
+        base = pl.multiple_of((rx // 2) * 256, 256)
+        lanes = pl.ds(pl.multiple_of(lax.rem(rx, 2) * 128, 128), 128)
+        for i, ref in enumerate((own_ref, other_ref)):
+            value = ref[pl.ds(rx, PQ, stride=RX), :]
+            if i == 0:
+                turned_ref[pl.ds(pl.multiple_of(rx * PQ_PAD, 8), PQ), :] = value
+            high, low = split(value)
+            for k, part in ((64 * i, high), (128 + 64 * i, low)):
+                rows = pl.ds(base + k + 48, 16)
+                data_ref[rows, lanes] = jnp.zeros((16, 128), bf16)
+                data_ref[pl.ds(base + k, PQ), lanes] = part
+        return carry
+
+    lax.fori_loop(0, RX, pack, 0, unroll=PACK_UNROLL)
 
     def pair(i, carry):
-        parts = []
-        for t in range(2):
-            rx = 2 * i + t
-            own = own_ref[pl.ds(rx, K_HALF, stride=RX), :]
-            other = other_ref[pl.ds(rx, K_HALF, stride=RX), :]
-            turned_ref[pl.ds(pl.multiple_of(rx * K_HALF, K_HALF), K_HALF), :] = own
-            own_high, own_low = split(own)
-            other_high, other_low = split(other)
-            parts.append(jnp.concatenate([own_high, other_high, own_low, other_low], axis=0))
-        data = jnp.concatenate(parts, axis=1)
+        data = data_ref[pl.ds(pl.multiple_of(i * 256, 256), 256), :]
         product = jnp.dot(wide_ref[...], data, preferred_element_type=f32)
         product = product + jnp.dot(narrow_ref[...], data[0:128], preferred_element_type=f32)
         for t in range(2):
@@ -230,14 +226,14 @@
             total = part[4 * PQ_PAD : 5 * PQ_PAD]
             for c in range(4):
                 total = total + shear_ref[pl.ds(4 * c + x, 1), :] * part[c * PQ_PAD : (c + 1) * PQ_PAD]
-            rate_ref[pl.ds(pl.multiple_of(rx * PQ_PAD, PQ_PAD), PQ_PAD), :] = total
+            rate_ref[pl.ds(pl.multiple_of(rx * PQ_PAD, 8), PQ_PAD), :] = total
         return carry
 
-    lax.fori_loop(0, N_PAIR, pair, 0)
-
-    def strip(j, carry):
+    lax.fori_loop(0, N_PAIR, pair, 0, unroll=PAIR_UNROLL)
+
+    def strip(j, count):
         def field(r, x):
-            return turned_ref[pl.ds(pl.multiple_of((4 * r + x) * K_HALF + 8 * j, 8), 8), :]
+            return turned_ref[pl.ds(pl.multiple_of((4 * r + x) * PQ_PAD + 8 * j, 8), 8), :]
 
         for x in range(4):
             def coef(i):
@@ -256,31 +252,29 @@
                         total = total + coef(i) * field(r, x + shift)
                 for shift, i in ((1, 5), (2, 6), (127, 7), (126, 8)):
                     total = total + coef(i) * pltpu.roll(f, shift, 1)
-                result_ref[pl.ds(j * (8 * RX) + 4 * r + x, 8, stride=RX), :] = total
+                out_ref[pl.ds(j * (8 * RX) + 4 * r + x, count, stride=RX), :] = total[0:count]
+
+    def whole(j, carry):
+        strip(j, 8)
         return carry
 
-    lax.fori_loop(0, PQ_PAD // 8, strip, 0)
-    copy_out = pltpu.make_async_copy(result_ref.at[0:ROWS], out_ref, sems.at[2])
-    copy_out.start()
-    copy_out.wait()
+    lax.fori_loop(0, PQ // 8, whole, 0, unroll=STRIP_UNROLL)
+    strip(PQ // 8, PQ % 8)
 
 
 def main(place, laguerre, own, other, velocity, shear, first, second, hermite):
     return pl.pallas_call(
         main_kernel,
-        in_specs=[smem, smem, hbm, hbm, vmem, vmem, vmem, vmem, vmem],
+        in_specs=[smem, smem] + [vmem] * 7,
         out_specs=vmem,
         out_shape=jax.ShapeDtypeStruct((ROWS, 128), f32),
         scratch_shapes=[
-            pltpu.VMEM((K_HALF * RX, 128), f32),
-            pltpu.VMEM((K_HALF * RX, 128), f32),
-            pltpu.VMEM((K_HALF * RX, 128), f32),
+            pltpu.VMEM((N_PAIR * 256, 256), bf16),
             pltpu.VMEM((PQ_PAD * RX, 128), f32),
             pltpu.VMEM((PQ_PAD * RX, 128), f32),
             pltpu.VMEM((5 * PQ_PAD, 256), bf16),
             pltpu.VMEM((5 * PQ_PAD, 128), bf16),
             pltpu.VMEM((9, 8, 128), f32),
-            pltpu.SemaphoreType.DMA((3,)),
         ],
         compiler_params=pltpu.CompilerParams(vmem_limit_bytes=24 << 20),
         cost_estimate=pl.CostEstimate(flops=2 * 280 * 384 * 5120, bytes_accessed=3 * ROWS * 512, transcendentals=0),

time: 43.4 us -> 40.3 us (0.929)
  the two profiles are of different devices: /device:TPU:257 before, /device:TPU:1 now
where the time goes in v2:
time: 40.3 us; the launch traced here: 40 us
  starting transfers between devices  21.5 us (53%)
  Pallas kernels  8.82 us (22%)
  blocking collectives  4.14 us (10%)
  waiting for transfers between devices  2.54 us (6%)
  local copies, waits for them, and re-layouts  2.2 us (5%)
  between operations  0.79 us (2%)
    ppermute x1, starting transfers between devices, body(): other = lax.ppermute(rows, 'col', [(0, 1), (1, 0)])  8.79 us
    ppermute x1, starting transfers between devices, body(): right = lax.ppermute(low, 'gx', back)  7.27 us
    pallas_call x1, Pallas kernels, main(): pl.pallas_call(main_kernel, in_specs=[smem, smem] + [vmem] * 7, out_specs...  5.83 us
    psum x1, blocking collectives, body(): stress = lax.psum(stress, 'col')  4.14 us
    ppermute x1, starting transfers between devices, body(): below = lax.ppermute(edge_high, 'gy', line)  2.09 us
    ppermute x1, starting transfers between devices, body(): left = lax.ppermute(high, 'gx', ring)  2.04 us
    unnamed x19, local copies, waits for them, and re-layouts  1.93 us
    ppermute x1, waiting for transfers between devices, body(): below = lax.ppermute(edge_high, 'gy', line)  1.48 us
  transfers between devices with their start and end apart: 5, of which 2 were waited for; matrix products, arithmetic and copies ran while one was open for 1% of the time, Pallas kernels for 18%

profile of v2, /device:TPU:1, one launch (start us, length us, event | category | flops | bytes accessed | tf_op | source)
XLA Modules:
  0.0 40.0 jit_solution(9645735715412804037)
XLA Ops:
  0.6 8.8 %collective-permute-start = (f32[2000,128]{1,0:T(8,128)}, f32[2000,128]{1,0:T(8,128)S(1)}, u32[]{:S(2)}, u32[]{:S(2)}) collective-permute-start(f32[2000,128]{1,0:T(8,128)} %bitcast.14), channel_id=1, source_target_pairs={{0,1},{1,0},{2,3},{3,2},{4,5},{5,4},{6,7},{7,6},{8,9},{9,8},{10,11... | collective-permute-start | bytes 3072008 | tf_op jit(solution)/shard_map/ppermute | solution.py:387
  9.4 0.0 copy-start
  9.4 1.2 %copy-done = f32[5,10,10,4,128]{4,3,2,1,0:T(4,128)S(1)} copy-done((f32[5,10,10,4,128]{4,3,2,1,0:T(4,128)S(1)}, f32[5,10,10,4,128]{4,3,2,1,0:T(4,128)}, u32[]{:S(2)}) %copy-start) | copy-done | bytes 1024024
  10.6 1.0 %x_halos.1 = (f32[5,2,104,128]{3,2,1,0:T(8,128)}, f32[5,2,104,128]{3,2,1,0:T(8,128)}) custom-call(f32[2000,128]{1,0:T(8,128)S(1)} %bitcast.15), custom_call_target="tpu_custom_call" | custom-call | bytes 2048000 | tf_op jit(solution)/shard_map/x_halos/pallas_call | solution.py:65
  11.7 2.0 %collective-permute-start.1 = (f32[5,2,104,128]{3,2,1,0:T(8,128)}, f32[5,2,104,128]{3,2,1,0:T(8,128)S(1)}, u32[]{:S(2)}, u32[]{:S(2)}) collective-permute-start(f32[5,2,104,128]{3,2,1,0:T(8,128)} %get-tuple-element.8), channel_id=1, source_target_pairs={{0,32},{32,64},{64,96},{96,128},{128,160},{160,192},{192,224},{224... | collective-permute-start | bytes 1597448 | tf_op jit(solution)/shard_map/ppermute | solution.py:382
  13.7 7.3 %collective-permute-start.2 = (f32[5,2,104,128]{3,2,1,0:T(8,128)}, f32[5,2,104,128]{3,2,1,0:T(8,128)S(1)}, u32[]{:S(2)}, u32[]{:S(2)}) collective-permute-start(f32[5,2,104,128]{3,2,1,0:T(8,128)} %get-tuple-element.9), channel_id=1, source_target_pairs={{32,0},{64,32},{96,64},{128,96},{160,128},{192,160},{224,192},{256... | collective-permute-start | bytes 1597448 | tf_op jit(solution)/shard_map/ppermute | solution.py:383
  21.0 0.5 %y_edges.1 = (f32[2,2560]{1,0:T(2,128)S(1)}, f32[2,2560]{1,0:T(2,128)S(1)}) custom-call(f32[2000,128]{1,0:T(8,128)S(1)} %bitcast.16), custom_call_target="tpu_custom_call" | custom-call | bytes 1024000 | tf_op jit(solution)/shard_map/y_edges/pallas_call | solution.py:94
  21.5 2.1 %collective-permute-start.3 = (f32[2,2560]{1,0:T(2,128)S(1)}, f32[2,2560]{1,0:T(2,128)S(1)}, u32[]{:S(2)}, u32[]{:S(2)}) collective-permute-start(f32[2,2560]{1,0:T(2,128)S(1)} %get-tuple-element.10), channel_id=1, source_target_pairs={{0,2},{2,4},{4,6},{6,8},{8,10},{10,12},{12,14},{14,16},{16,18},{18... | collective-permute-start | bytes 61448 | tf_op jit(solution)/shard_map/ppermute | solution.py:385
  23.6 1.3 %collective-permute-start.4 = (f32[2,2560]{1,0:T(2,128)S(1)}, f32[2,2560]{1,0:T(2,128)S(1)}, u32[]{:S(2)}, u32[]{:S(2)}) collective-permute-start(f32[2,2560]{1,0:T(2,128)S(1)} %get-tuple-element.11), channel_id=1, source_target_pairs={{2,0},{4,2},{6,4},{8,6},{10,8},{12,10},{14,12},{16,14},{18,16},{20... | collective-permute-start | bytes 61448 | tf_op jit(solution)/shard_map/ppermute | solution.py:386
  24.9 0.0 copy-done.8
  24.9 0.1 reshape.34
  25.0 0.0 copy-start.3
  25.0 0.0 copy-start.4
  25.1 0.0 copy-start.5
  25.1 0.0 copy-start.6
  25.1 0.0 copy-start.7
  25.1 0.2 copy.12
  25.3 0.0 collective-permute-done.other_ref
  25.3 0.0 copy-start.2
  25.3 0.0 copy-done.1
  25.3 0.5 %copy-done.3 = f32[4,10,10]{2,0,1:T(4,128)S(1)} copy-done((f32[4,10,10]{2,0,1:T(4,128)S(1)}, f32[4,10,10]{2,0,1:T(4,128)}, u32[]{:S(2)}) %copy-start.3) | copy-done | bytes 1624
  25.8 0.0 copy-done.4
  25.8 0.0 copy-done.5
  25.8 0.0 copy-done.7
  25.8 0.2 copy-done.2
  26.0 5.8 %main_step.1.partial_ref = f32[2000,128]{1,0:T(8,128)S(1)} custom-call(s32[1]{0:T(128)} %bitcast.place_ref, f32[10,10]{1,0:T(8,128)S(1)} %copy-done.5, f32[2000,128]{1,0:T(8,128)S(1)} %bitcast.17, f32[2000,128]{1,0:T(8,128)S(1)} %collective-permute-done.other_ref, f32[8,128]{1,0:T(8,128)S(1)} %bitcast.19, f32[16,128]{1,0:T(8,128)S(1)} %bitcast.23, ...), custom_call_target="tpu_custom_call" | custom-call | flops 1101004800 | bytes 3072000 | tf_op jit(solution)/shard_map/main_step/pallas_call | solution.py:266
  31.8 1.5 %collective-permute-done.3.below_ref = f32[2,2560]{1,0:T(2,128)S(1)} collective-permute-done((f32[2,2560]{1,0:T(2,128)S(1)}, f32[2,2560]{1,0:T(2,128)S(1)}, u32[]{:S(2)}, u32[]{:S(2)}) %collective-permute-start.3) | collective-permute-done | bytes 20512 | tf_op jit(solution)/shard_map/ppermute | solution.py:385
  33.3 1.0 %collective-permute-done.4.above_ref = f32[2,2560]{1,0:T(2,128)S(1)} collective-permute-done((f32[2,2560]{1,0:T(2,128)S(1)}, f32[2,2560]{1,0:T(2,128)S(1)}, u32[]{:S(2)}, u32[]{:S(2)}) %collective-permute-start.4) | collective-permute-done | bytes 20512 | tf_op jit(solution)/shard_map/ppermute | solution.py:386
  34.3 0.0 collective-permute-done.1.left_ref
  34.4 0.0 collective-permute-done.2.right_ref
  34.4 1.5 %final_step.1 = (f32[2000,128]{1,0:T(8,128)}, f32[3,4,128]{2,1,0:T(4,128)S(1)}) custom-call(f32[2000,128]{1,0:T(8,128)S(1)} %main_step.1.partial_ref, f32[5,2,104,128]{3,2,1,0:T(8,128)S(1)} %collective-permute-done.1.left_ref, f32[5,2,104,128]{3,2,1,0:T(8,128)S(1)} %collective-permute-done.2.right_ref, f32[2,2560]{1,0:T(2,128)S(1)} %collective-permute-done.3.below_ref, ...), custom_call_target="tpu_custom_call" | custom-call | flops 5120000 | bytes 4096000 | tf_op jit(solution)/shard_map/final_step/pallas_call | solution.py:344
  35.8 4.1 %psum.7 = f32[3,4,128]{2,1,0:T(4,128)} all-reduce(f32[3,4,128]{2,1,0:T(4,128)S(1)} %get-tuple-element.13), channel_id=1, replica_groups=mesh['gx'=16,'gy'=16,'col'=2] {'col'}, use_global_device_ids=true, to_apply=%region_0.0 | all-reduce | flops 1536 | bytes 12288 | tf_op jit(solution)/shard_map/psum | solution.py:390
  (4 shorter events, 0.0 us)
Async XLA Ops:
  0.6 24.6 %collective-permute-start = (f32[2000,128]{1,0:T(8,128)}, f32[2000,128]{1,0:T(8,128)S(1)}, u32[]{:S(2)}, u32[]{:S(2)}) collective-permute-start(f32[2000,128]{1,0:T(8,128)} %bitcast.14), channel_id=1, source_target_pairs={{0,1},{1,0},{2,3},{3,2},{4,5},{5,4},{6,7},{7,6},{8,9},{9,8},{10,11... | collective-permute-start | bytes 3072008 | tf_op jit(solution)/shard_map/ppermute | solution.py:387
  9.4 1.2 %copy-start = (f32[5,10,10,4,128]{4,3,2,1,0:T(4,128)S(1)}, f32[5,10,10,4,128]{4,3,2,1,0:T(4,128)}, u32[]{:S(2)}) copy-start(f32[5,10,10,4,128]{4,3,2,1,0:T(4,128)} %param.8) | copy-start | bytes 3072004
  10.6 14.3 %copy-start.8 = (f32[3,5,10,10]{3,0,2,1:T(4,128)S(1)}, f32[3,5,10,10]{3,0,2,1:T(4,128)}, u32[]{:S(2)}) copy-start(f32[3,5,10,10]{3,0,2,1:T(4,128)} %param.15) | copy-start | bytes 18004
  11.7 13.6 %copy-start.1 = (f32[5,10,10,4,128]{4,3,2,1,0:T(4,128)S(1)}, f32[5,10,10,4,128]{4,3,2,1,0:T(4,128)}, u32[]{:S(2)}) copy-start(f32[5,10,10,4,128]{4,3,2,1,0:T(4,128)} %param.8) | copy-start | bytes 3072004
  11.7 22.7 %collective-permute-start.1 = (f32[5,2,104,128]{3,2,1,0:T(8,128)}, f32[5,2,104,128]{3,2,1,0:T(8,128)S(1)}, u32[]{:S(2)}, u32[]{:S(2)}) collective-permute-start(f32[5,2,104,128]{3,2,1,0:T(8,128)} %get-tuple-element.8), channel_id=1, source_target_pairs={{0,32},{32,64},{64,96},{96,128},{128,160},{160,192},{192,224},{224... | collective-permute-start | bytes 1597448 | tf_op jit(solution)/shard_map/ppermute | solution.py:382
  13.7 20.6 %collective-permute-start.2 = (f32[5,2,104,128]{3,2,1,0:T(8,128)}, f32[5,2,104,128]{3,2,1,0:T(8,128)S(1)}, u32[]{:S(2)}, u32[]{:S(2)}) collective-permute-start(f32[5,2,104,128]{3,2,1,0:T(8,128)} %get-tuple-element.9), channel_id=1, source_target_pairs={{32,0},{64,32},{96,64},{128,96},{160,128},{192,160},{224,192},{256... | collective-permute-start | bytes 1597448 | tf_op jit(solution)/shard_map/ppermute | solution.py:383
  21.5 11.8 %collective-permute-start.3 = (f32[2,2560]{1,0:T(2,128)S(1)}, f32[2,2560]{1,0:T(2,128)S(1)}, u32[]{:S(2)}, u32[]{:S(2)}) collective-permute-start(f32[2,2560]{1,0:T(2,128)S(1)} %get-tuple-element.10), channel_id=1, source_target_pairs={{0,2},{2,4},{4,6},{6,8},{8,10},{10,12},{12,14},{14,16},{16,18},{18... | collective-permute-start | bytes 61448 | tf_op jit(solution)/shard_map/ppermute | solution.py:385
  23.6 10.7 %collective-permute-start.4 = (f32[2,2560]{1,0:T(2,128)S(1)}, f32[2,2560]{1,0:T(2,128)S(1)}, u32[]{:S(2)}, u32[]{:S(2)}) collective-permute-start(f32[2,2560]{1,0:T(2,128)S(1)} %get-tuple-element.11), channel_id=1, source_target_pairs={{2,0},{4,2},{6,4},{8,6},{10,8},{12,10},{14,12},{16,14},{18,16},{20... | collective-permute-start | bytes 61448 | tf_op jit(solution)/shard_map/ppermute | solution.py:386
  25.0 0.7 %copy-start.3 = (f32[4,10,10]{2,0,1:T(4,128)S(1)}, f32[4,10,10]{2,0,1:T(4,128)}, u32[]{:S(2)}) copy-start(f32[4,10,10]{2,0,1:T(4,128)} %param.13) | copy-start | bytes 4804
  25.0 0.7 %copy-start.4 = (f32[4,10,10]{2,0,1:T(4,128)S(1)}, f32[4,10,10]{2,0,1:T(4,128)}, u32[]{:S(2)}) copy-start(f32[4,10,10]{2,0,1:T(4,128)} %param.14) | copy-start | bytes 4804
  25.1 0.7 %copy-start.5 = (f32[10,10]{1,0:T(8,128)S(1)}, f32[10,10]{1,0:T(8,128)}, u32[]{:S(2)}) copy-start(f32[10,10]{1,0:T(8,128)} %laguerre_ref.1) | copy-start | bytes 1204
  25.1 0.7 %copy-start.6 = (f32[4,4,128]{2,1,0:T(4,128)S(1)}, f32[4,4,128]{2,1,0:T(4,128)}, u32[]{:S(2)}) copy-start(f32[4,4,128]{2,1,0:T(4,128)} %param.10) | copy-start | bytes 24580
  25.1 0.7 %copy-start.7 = (f32[10,10]{1,0:T(8,128)S(1)}, f32[10,10]{1,0:T(8,128)}, u32[]{:S(2)}) copy-start(f32[10,10]{1,0:T(8,128)} %hermite_ref.1) | copy-start | bytes 1204
  25.3 0.7 %copy-start.2 = (f32[2,4,128]{2,1,0:T(4,128)S(1)}, f32[2,4,128]{2,1,0:T(4,128)}, u32[]{:S(2)}) copy-start(f32[2,4,128]{2,1,0:T(4,128)} %param.9) | copy-start | bytes 12292

commit v3 on v2

--- a/solution.py
+++ b/solution.py
@@ -19,14 +19,12 @@
 K_HALF = 64
 N_PAIR = 20
 MODES_P = 100
-MODES_PAD = 104
 PACK_UNROLL = 40
 PAIR_UNROLL = 20
 STRIP_UNROLL = 1
 
 
 vmem = pl.BlockSpec(memory_space=pltpu.VMEM)
-smem = pl.BlockSpec(memory_space=pltpu.SMEM)
 hbm = pl.BlockSpec(memory_space=pl.ANY)
 
 
@@ -53,15 +51,16 @@
     return jnp.where(condition, 1.0, 0.0).astype(f32)
 
 
-def halo_kernel(x_ref, low_ref, high_ref):
-    for p in range(5):
-        for k in range(2):
-            low_ref[p, k, 0:MODES_P, :] = x_ref[pl.ds(400 * p + k, MODES_P, stride=4), :]
-            high_ref[p, k, 0:MODES_P, :] = x_ref[pl.ds(400 * p + 2 + k, MODES_P, stride=4), :]
+def halo_kernel(x_ref, one_ref, two_ref):
+    odd = 1 - lax.rem(lax.axis_index("gx"), 2)
+    for ref, offset in ((one_ref, 2 - 2 * odd), (two_ref, 2 * odd)):
+        for p in range(5):
+            for k in range(2):
+                ref[pl.ds(MODES_P * (2 * p + k), MODES_P), :] = x_ref[pl.ds(400 * p + k + offset, MODES_P, stride=4), :]
 
 
 def x_halos(rows):
-    shape = jax.ShapeDtypeStruct((5, 2, MODES_PAD, 128), f32)
+    shape = jax.ShapeDtypeStruct((ROWS // 2, 128), f32)
     return pl.pallas_call(
         halo_kernel,
         in_specs=[vmem],
@@ -73,11 +72,15 @@
     )(rows)
 
 
-def edge_kernel(x_ref, low_ref, high_ref, rows_ref):
+def edge_kernel(x_ref, *refs):
+    small, (one_ref, two_ref), kept, (rows_ref,) = refs[:6], refs[6:8], refs[8:14], refs[14:]
+    for source, target in zip(small, kept):
+        target[...] = source[...]
     for x in range(4):
         rows_ref[x * 128 + 96 : (x + 1) * 128, :] = jnp.zeros((32, 256), bf16)
     lane = lax.rem(iota((8, 256), 1), 128)
     row = iota((8, 256), 0)
+    row = jnp.where(lax.rem(lax.axis_index("gy"), 2) == 0, jnp.bitwise_xor(row, 2), row)
     pick = one_hot(((row < 2) & (lane == row)) | ((row >= 2) & (row < 4) & (lane == row + 124))).astype(bf16)
     for p in range(5):
         for x in range(4):
@@ -85,28 +88,37 @@
             rows_ref[x * 128 : x * 128 + MODES_P, 0:128] = high
             rows_ref[x * 128 : x * 128 + MODES_P, 128:256] = low
         edges = lax.dot_general(pick, rows_ref[...], (((1,), (1,)), ((), ())), preferred_element_type=f32)
-        low_ref[:, p * 512 : (p + 1) * 512] = edges[0:2]
-        high_ref[:, p * 512 : (p + 1) * 512] = edges[2:4]
-
-
-def y_edges(rows):
+        one_ref[:, p * 512 : (p + 1) * 512] = edges[0:2]
+        two_ref[:, p * 512 : (p + 1) * 512] = edges[2:4]
+
+
+def y_edges(rows, small):
     shape = jax.ShapeDtypeStruct((2, 5 * 512), f32)
-    return pl.pallas_call(
+    outs = pl.pallas_call(
         edge_kernel,
-        in_specs=[vmem],
-        out_specs=[vmem, vmem],
-        out_shape=[shape, shape],
+        in_specs=[vmem] * 7,
+        out_specs=[vmem] * 8,
+        out_shape=[shape, shape] + [jax.ShapeDtypeStruct(a.shape, f32) for a in small],
         scratch_shapes=[pltpu.VMEM((512, 256), bf16)],
         cost_estimate=pl.CostEstimate(flops=0, bytes_accessed=ROWS * 512, transcendentals=0),
         compiler_params=pltpu.CompilerParams(vmem_limit_bytes=16 << 20),
         name="y_edges",
-    )(rows)
+    )(rows, *small)
+    return outs[0], outs[1], outs[2:]
 
 
 def split(value):
     high = value.astype(bf16)
     low = (value - high.astype(f32)).astype(bf16)
     return high, low
+
+
+def exact(pick, table):
+    high, low = split(table)
+    rest = (table - high.astype(f32) - low.astype(f32)).astype(bf16)
+    total = jnp.dot(pick, high, preferred_element_type=f32)
+    total = total + jnp.dot(pick, low, preferred_element_type=f32)
+    return total + jnp.dot(pick, rest, preferred_element_type=f32)
 
 
 def coupling(start, first, second, hermite):
@@ -121,19 +133,6 @@
         a = tens(ab)
         return c, a + start, ab - 10 * a, ab < PQ
 
-    def expand(table, index, c, valid):
-        t40 = iota((rows, 40), 1)
-        t10 = iota((rows, 10), 1)
-        c40, a40, b40, ok40 = row_ids(40)
-        c10, a10, b10, ok10 = row_ids(10)
-        i40 = a40 if index == 0 else b40
-        i10 = a10 if index == 0 else b10
-        pick_flow = one_hot(ok40 & (c40 < 4) & (t40 == 4 * i40 + c40))
-        pick_spring = one_hot(ok10 & (c10 == 4) & (t10 == i10))
-        return jnp.dot(pick_flow, table, precision=highest, preferred_element_type=f32) + jnp.dot(
-            pick_spring, hermite, precision=highest, preferred_element_type=f32
-        )
-
     def columns(height):
         k = iota((height, 128), 1)
         other = k >= K_HALF
@@ -142,14 +141,29 @@
         p = p_here + jnp.where(other, 5 - start, start)
         return p, kk - 10 * p_here, kk < PQ
 
-    c, a, b, valid = row_ids(128)
     p10, q10, ok10 = columns(10)
     source = iota((10, 128), 0)
-    left = expand(first, 0, c, valid)
-    right = expand(second, 1, c, valid)
-    left = jnp.dot(left, one_hot(ok10 & (source == p10)), precision=highest, preferred_element_type=f32)
-    right = jnp.dot(right, one_hot(ok10 & (source == q10)), precision=highest, preferred_element_type=f32)
-    p, q, ok = columns(rows)
+    spread_p = one_hot(ok10 & (source == p10))
+    spread_q = one_hot(ok10 & (source == q10))
+
+    def table(flow, spread):
+        return jnp.concatenate(
+            [
+                jnp.dot(flow, spread, precision=highest, preferred_element_type=f32),
+                jnp.dot(hermite, spread, precision=highest, preferred_element_type=f32),
+                jnp.zeros((6, 128), f32),
+            ],
+            axis=0,
+        )
+
+    c, a, b, valid = row_ids(56)
+    t = iota((rows, 56), 1)
+    pick_a = one_hot(valid & (t == jnp.where(c == 4, 40 + a, 4 * a + c))).astype(bf16)
+    pick_b = one_hot(valid & (t == jnp.where(c == 4, 40 + b, 4 * b + c))).astype(bf16)
+    left = exact(pick_a, table(first, spread_p))
+    right = exact(pick_b, table(second, spread_q))
+    c, a, b, _ = row_ids(128)
+    p, q, _ = columns(rows)
     spring = c == 4
     both = left * jnp.where(spring, one_hot(b == q), right)
     both = both + jnp.where(spring & (a == p), right, 0.0)
@@ -157,7 +171,6 @@
 
 
 def main_kernel(
-    place_ref,
     laguerre_ref,
     own_ref,
     other_ref,
@@ -173,8 +186,9 @@
     wide_ref,
     narrow_ref,
     coef_ref,
+    mix_ref,
 ):
-    matrix = coupling(place_ref[0], first_ref[...], second_ref[...], hermite_ref[...])
+    matrix = coupling(5 * lax.axis_index("col"), first_ref[...], second_ref[...], hermite_ref[...])
     matrix_high, matrix_low = split(matrix)
     wide_ref[:, 0:128] = matrix_high
     wide_ref[:, 128:256] = matrix_high
@@ -198,6 +212,10 @@
     )
     for i, c in enumerate(coefs):
         coef_ref[i, 0:4, :] = c
+    laguerre = time_step * laguerre_ref[...]
+    for r in range(10):
+        for s in range(10):
+            mix_ref[10 * r + s] = jnp.broadcast_to(laguerre[r : r + 1, s : s + 1], (8, 128))
 
     def pack(rx, carry):
         base = pl.multiple_of((rx // 2) * 256, 256)
@@ -235,24 +253,25 @@
         def field(r, x):
             return turned_ref[pl.ds(pl.multiple_of((4 * r + x) * PQ_PAD + 8 * j, 8), 8), :]
 
-        for x in range(4):
-            def coef(i):
-                return coef_ref[i, x : x + 1, :]
-
-            here = [field(r, x) for r in range(10)]
+        def coef(i, x):
+            return coef_ref[i, x : x + 1, :]
+
+        for half in ((0, 1), (2, 3)):
+            here = {x: [field(r, x) for r in range(10)] for x in half}
             for r in range(10):
-                mixed = laguerre_ref[r, 0] * here[0]
-                for s in range(1, 10):
-                    mixed = mixed + laguerre_ref[r, s] * here[s]
-                f = here[r]
-                total = rate_ref[pl.ds(pl.multiple_of((4 * r + x) * PQ_PAD + 8 * j, 8), 8), :]
-                total = total + time_step * mixed + coef(0) * f
-                for shift, i in ((-1, 1), (-2, 2), (1, 3), (2, 4)):
-                    if 0 <= x + shift < 4:
-                        total = total + coef(i) * field(r, x + shift)
-                for shift, i in ((1, 5), (2, 6), (127, 7), (126, 8)):
-                    total = total + coef(i) * pltpu.roll(f, shift, 1)
-                out_ref[pl.ds(j * (8 * RX) + 4 * r + x, count, stride=RX), :] = total[0:count]
+                mix = [mix_ref[10 * r + s] for s in range(10)]
+                for x in half:
+                    f = here[x][r]
+                    total = rate_ref[pl.ds(pl.multiple_of((4 * r + x) * PQ_PAD + 8 * j, 8), 8), :]
+                    total = total + coef(0, x) * f
+                    for s in range(10):
+                        total = total + mix[s] * here[x][s]
+                    for shift, i in ((-1, 1), (-2, 2), (1, 3), (2, 4)):
+                        if 0 <= x + shift < 4:
+                            total = total + coef(i, x) * field(r, x + shift)
+                    for shift, i in ((1, 5), (2, 6), (127, 7), (126, 8)):
+                        total = total + coef(i, x) * pltpu.roll(f, shift, 1)
+                    out_ref[pl.ds(j * (8 * RX) + 4 * r + x, count, stride=RX), :] = total[0:count]
 
     def whole(j, carry):
         strip(j, 8)
@@ -262,10 +281,10 @@
     strip(PQ // 8, PQ % 8)
 
 
-def main(place, laguerre, own, other, velocity, shear, first, second, hermite):
+def main(laguerre, own, other, velocity, shear, first, second, hermite):
     return pl.pallas_call(
         main_kernel,
-        in_specs=[smem, smem] + [vmem] * 7,
+        in_specs=[vmem] * 8,
         out_specs=vmem,
         out_shape=jax.ShapeDtypeStruct((ROWS, 128), f32),
         scratch_shapes=[
@@ -275,16 +294,35 @@
             pltpu.VMEM((5 * PQ_PAD, 256), bf16),
             pltpu.VMEM((5 * PQ_PAD, 128), bf16),
             pltpu.VMEM((9, 8, 128), f32),
+            pltpu.VMEM((100, 8, 128), f32),
         ],
         compiler_params=pltpu.CompilerParams(vmem_limit_bytes=24 << 20),
         cost_estimate=pl.CostEstimate(flops=2 * 280 * 384 * 5120, bytes_accessed=3 * ROWS * 512, transcendentals=0),
         name="main_step",
-    )(place, laguerre, own, other, velocity, shear, first, second, hermite)
+    )(laguerre, own, other, velocity, shear, first, second, hermite)
 
 
 def final_kernel(
-    partial_ref, left_ref, right_ref, below_ref, above_ref, velocity_ref, weight_ref, out_hbm, stress_ref, out_ref, sems
+    partial_ref,
+    x_one_ref,
+    x_two_ref,
+    y_one_ref,
+    y_two_ref,
+    velocity_ref,
+    weight_ref,
+    out_hbm,
+    stress_ref,
+    out_ref,
+    sems,
 ):
+    odd_x = lax.rem(lax.axis_index("gx"), 2) == 0
+    odd_y = lax.rem(lax.axis_index("gy"), 2) == 1
+
+    def halo(on_left, p, k):
+        layer = pl.ds(MODES_P * (2 * p + k), MODES_P)
+        one, two = x_one_ref[layer, :], x_two_ref[layer, :]
+        return jnp.where(odd_x, one, two) if on_left else jnp.where(odd_x, two, one)
+
     u = velocity_ref[0:4, :]
     v = velocity_ref[4:8, :]
     lane4 = iota((4, 128), 1)
@@ -303,17 +341,21 @@
     copies = []
     for p in range(5):
         lanes = slice(p * 512, (p + 1) * 512)
-        edges = jnp.concatenate([below_ref[:, lanes], above_ref[:, lanes], jnp.zeros((4, 512), f32)], axis=0)
+        y_one = y_one_ref[:, lanes]
+        y_two = y_two_ref[:, lanes]
+        below = jnp.where(odd_y, y_one, y_two)
+        above = jnp.where(odd_y, y_two, y_one)
+        edges = jnp.concatenate([below, above, jnp.zeros((4, 512), f32)], axis=0)
         high = edges.astype(bf16).astype(f32)
         rest = edges - high
         middle = rest.astype(bf16).astype(f32)
         low = rest - middle
         stacked = jnp.concatenate([high, middle, low, jnp.zeros((8, 512), f32)], axis=0).astype(bf16)
         spread = lax.dot_general(stacked, place, (((0,), (0,)), ((), ())), preferred_element_type=f32)
-        left_far = left_ref[p, 0, 0:MODES_P, :]
-        left_near = left_ref[p, 1, 0:MODES_P, :]
-        right_near = right_ref[p, 0, 0:MODES_P, :]
-        right_far = right_ref[p, 1, 0:MODES_P, :]
+        left_far = halo(True, p, 0)
+        left_near = halo(True, p, 1)
+        right_near = halo(False, p, 0)
+        right_far = halo(False, p, 1)
         for x in range(4):
             total = partial_ref[pl.ds(400 * p + x, MODES_P, stride=4), :]
             total = total + near[x : x + 1] * spread[x * 128 : x * 128 + MODES_P, 0:128]
@@ -340,7 +382,7 @@
         copy.wait()
 
 
-def final(partial, left, right, below, above, velocity, weights):
+def final(partial, x_one, x_two, y_one, y_two, velocity, weights):
     return pl.pallas_call(
         final_kernel,
         in_specs=[vmem] * 7,
@@ -350,7 +392,7 @@
         cost_estimate=pl.CostEstimate(flops=20 * ROWS * 128, bytes_accessed=4 * ROWS * 512, transcendentals=0),
         compiler_params=pltpu.CompilerParams(vmem_limit_bytes=16 << 20),
         name="final_step",
-    )(partial, left, right, below, above, velocity, weights)
+    )(partial, x_one, x_two, y_one, y_two, velocity, weights)
 
 
 def body(
@@ -369,24 +411,25 @@
     first = jnp.transpose(flow_first, (1, 0, 2)).reshape(40, 10)
     second = jnp.transpose(flow_second, (1, 0, 2)).reshape(40, 10)
     weights = jnp.transpose(stress_weights.reshape(3, 5, MODES_P), (1, 2, 0))
-    place = (lax.axis_index("col") * 5).astype(jnp.int32).reshape(1)
-
-    count_x = lax.axis_size("gx")
-    count_y = lax.axis_size("gy")
-    ring = [(i, (i + 1) % count_x) for i in range(count_x)]
-    back = [(target, source) for source, target in ring]
-    line = [(i, i + 1) for i in range(count_y - 1)]
-    line_back = [(target, source) for source, target in line]
-
-    low, high = x_halos(rows)
-    left = lax.ppermute(high, "gx", ring)
-    right = lax.ppermute(low, "gx", back)
-    edge_low, edge_high = y_edges(rows)
-    below = lax.ppermute(edge_high, "gy", line)
-    above = lax.ppermute(edge_low, "gy", line_back)
+    def pairings(axis, periodic):
+        count = lax.axis_size(axis)
+        one = [(i, i + 1) for i in range(0, count, 2)]
+        two = [(i, (i + 1) % count) for i in range(1, count if periodic else count - 1, 2)]
+        return [pairs + [(b, a) for a, b in pairs] for pairs in (one, two)]
+
+    ring_two, ring_one = pairings("gx", True)
+    line_one, line_two = pairings("gy", False)
+    send_one, send_two = x_halos(rows)
+    x_one = lax.ppermute(send_one, "gx", ring_one)
+    x_two = lax.ppermute(send_two, "gx", ring_two)
+    small = (speeds, shear, first, second, hermite_matrix, laguerre_matrix)
+    send_one, send_two, small = y_edges(rows, small)
+    speeds, shear, first, second, hermite_matrix, laguerre_matrix = small
+    y_one = lax.ppermute(send_one, "gy", line_one)
+    y_two = lax.ppermute(send_two, "gy", line_two)
     other = lax.ppermute(rows, "col", [(0, 1), (1, 0)])
-    partial = main(place, laguerre_matrix, rows, other, speeds, shear, first, second, hermite_matrix)
-    advanced, stress = final(partial, left, right, below, above, speeds, weights)
+    partial = main(laguerre_matrix, rows, other, speeds, shear, first, second, hermite_matrix)
+    advanced, stress = final(partial, x_one, x_two, y_one, y_two, speeds, weights)
     stress = lax.psum(stress, "col")
     return (advanced.reshape(density.shape), stress)
 

time: 40.3 us -> 37.7 us (0.935)
  the two profiles are of different devices: /device:TPU:1 before, /device:TPU:259 now
where the time goes in v3:
time: 37.7 us; the launch traced here: 37.4 us
  starting transfers between devices  20.6 us (55%)
  Pallas kernels  7.39 us (20%)
  blocking collectives  4.74 us (13%)
  waiting for transfers between devices  2.37 us (6%)
  local copies, waits for them, and re-layouts  1.53 us (4%)
  between operations  0.82 us (2%)
    ppermute x1, starting transfers between devices, body(): x_two = lax.ppermute(send_two, 'gx', ring_two)  6.47 us
    ppermute x1, starting transfers between devices, body(): y_one = lax.ppermute(send_one, 'gy', line_one)  4.76 us
    psum x1, blocking collectives, body(): stress = lax.psum(stress, 'col')  4.74 us
    pallas_call x1, Pallas kernels, main(): pl.pallas_call(main_kernel, in_specs=[vmem] * 8, out_specs=vmem, out_shap...  4.31 us
    ppermute x1, starting transfers between devices, body(): y_two = lax.ppermute(send_two, 'gy', line_two)  3.52 us
    ppermute x1, starting transfers between devices, body(): x_one = lax.ppermute(send_one, 'gx', ring_one)  3.24 us
    ppermute x1, starting transfers between devices, body(): other = lax.ppermute(rows, 'col', [(0, 1), (1, 0)])  2.59 us
    ppermute x1, waiting for transfers between devices, body(): y_two = lax.ppermute(send_two, 'gy', line_two)  2.36 us
  transfers between devices with their start and end apart: 5, of which 1 were waited for; matrix products, arithmetic and copies ran while one was open for 1% of the time, Pallas kernels for 16%

profile of v3, /device:TPU:259, one launch (start us, length us, event | category | flops | bytes accessed | tf_op | source)
XLA Modules:
  0.0 37.4 jit_solution(16198134427862027860)
XLA Ops:
  0.6 2.6 %collective-permute-start = (f32[2000,128]{1,0:T(8,128)}, f32[2000,128]{1,0:T(8,128)S(1)}, u32[]{:S(2)}, u32[]{:S(2)}) collective-permute-start(f32[2000,128]{1,0:T(8,128)} %bitcast.13), channel_id=1, source_target_pairs={{0,1},{1,0},{2,3},{3,2},{4,5},{5,4},{6,7},{7,6},{8,9},{9,8},{10,11... | collective-permute-start | bytes 3072008 | tf_op jit(solution)/shard_map/ppermute | solution.py:430
  3.2 0.0 copy-start
  3.2 1.2 %copy-done = f32[5,10,10,4,128]{4,3,2,1,0:T(4,128)S(1)} copy-done((f32[5,10,10,4,128]{4,3,2,1,0:T(4,128)S(1)}, f32[5,10,10,4,128]{4,3,2,1,0:T(4,128)}, u32[]{:S(2)}) %copy-start) | copy-done | bytes 1024024
  4.4 0.0 copy-start.2
  4.4 0.0 copy-start.3
  4.5 0.0 copy-start.6
  4.5 0.0 copy-start.7
  4.5 0.0 copy-start.8
  4.5 1.1 %x_halos.1 = (f32[1000,128]{1,0:T(8,128)}, f32[1000,128]{1,0:T(8,128)}) custom-call(f32[2000,128]{1,0:T(8,128)S(1)} %bitcast.14), custom_call_target="tpu_custom_call" | custom-call | bytes 2048000 | tf_op jit(solution)/shard_map/x_halos/pallas_call | solution.py:64
  5.6 3.2 %collective-permute-start.1 = (f32[1000,128]{1,0:T(8,128)}, f32[1000,128]{1,0:T(8,128)S(1)}, u32[]{:S(2)}, u32[]{:S(2)}) collective-permute-start(f32[1000,128]{1,0:T(8,128)} %get-tuple-element.20), channel_id=1, source_target_pairs={{32,64},{96,128},{160,192},{224,256},{288,320},{352,384},{416,448}... | collective-permute-start | bytes 1536008 | tf_op jit(solution)/shard_map/ppermute | solution.py:423
  8.8 6.5 %collective-permute-start.2 = (f32[1000,128]{1,0:T(8,128)}, f32[1000,128]{1,0:T(8,128)S(1)}, u32[]{:S(2)}, u32[]{:S(2)}) collective-permute-start(f32[1000,128]{1,0:T(8,128)} %get-tuple-element.21), channel_id=1, source_target_pairs={{0,32},{64,96},{128,160},{192,224},{256,288},{320,352},{384,416},{... | collective-permute-start | bytes 1536008 | tf_op jit(solution)/shard_map/ppermute | solution.py:424
  15.3 0.0 copy-done.2
  15.3 0.0 copy-done.3
  15.3 0.0 copy-done.4
  15.3 0.0 copy-done.5
  15.3 0.0 copy-done.6
  15.3 0.0 copy-done.7
  15.3 0.5 %y_edges.1 = (f32[2,2560]{1,0:T(2,128)S(1)}, f32[2,2560]{1,0:T(2,128)S(1)}, f32[8,128]{1,0:T(8,128)S(1)}, f32[16,128]{1,0:T(8,128)S(1)}, f32[40,10]{1,0:T(8,128)...) custom-call(f32[2000,128]{1,0:T(8,128)S(1)} %bitcast.15, f32[8,128]{1,0:T(8,128)S(1)} %bitcast.21, ...), custom_call_target="tpu_custom_call" | custom-call | bytes 1024000 | tf_op jit(solution)/shard_map/y_edges/pallas_call | solution.py:97
  15.8 4.8 %collective-permute-start.3 = (f32[2,2560]{1,0:T(2,128)S(1)}, f32[2,2560]{1,0:T(2,128)S(1)}, u32[]{:S(2)}, u32[]{:S(2)}) collective-permute-start(f32[2,2560]{1,0:T(2,128)S(1)} %get-tuple-element.22), channel_id=1, source_target_pairs={{0,2},{4,6},{8,10},{12,14},{16,18},{20,22},{24,26},{28,30},{2,0},{... | collective-permute-start | bytes 61448 | tf_op jit(solution)/shard_map/ppermute | solution.py:428
  20.6 3.5 %collective-permute-start.4 = (f32[2,2560]{1,0:T(2,128)S(1)}, f32[2,2560]{1,0:T(2,128)S(1)}, u32[]{:S(2)}, u32[]{:S(2)}) collective-permute-start(f32[2,2560]{1,0:T(2,128)S(1)} %get-tuple-element.23), channel_id=1, source_target_pairs={{2,4},{6,8},{10,12},{14,16},{18,20},{22,24},{26,28},{4,2},{8,6},{1... | collective-permute-start | bytes 61448 | tf_op jit(solution)/shard_map/ppermute | solution.py:429
  24.1 0.0 copy-done.8
  24.2 0.1 reshape.30
  24.3 0.2 copy.12
  24.5 0.0 collective-permute-done.other_ref
  24.5 0.0 copy-done.1
  24.5 4.3 %main_step.1.partial_ref = f32[2000,128]{1,0:T(8,128)S(1)} custom-call(f32[10,10]{1,0:T(8,128)S(1)} %get-tuple-element.14.laguerre_ref, f32[2000,128]{1,0:T(8,128)S(1)} %bitcast.16, f32[2000,128]{1,0:T(8,128)S(1)} %collective-permute-done.other_ref, f32[8,128]{1,0:T(8,128)S(1)} %get-tuple-element.15.velocity_ref, f32[16,128]{1,0:T(8,128)S(1)} %get-tuple-element.16.shear_ref, ...), custom_call_target="tpu_custom_call" | custom-call | flops 1101004800 | bytes 3072000 | tf_op jit(solution)/shard_map/main_step/pallas_call | solution.py:285
  28.8 0.0 collective-permute-done.3.y_one_ref
  28.8 2.4 %collective-permute-done.4.y_two_ref = f32[2,2560]{1,0:T(2,128)S(1)} collective-permute-done((f32[2,2560]{1,0:T(2,128)S(1)}, f32[2,2560]{1,0:T(2,128)S(1)}, u32[]{:S(2)}, u32[]{:S(2)}) %collective-permute-start.4) | collective-permute-done | bytes 20512 | tf_op jit(solution)/shard_map/ppermute | solution.py:429
  31.2 0.0 collective-permute-done.1.x_one_ref
  31.2 0.0 collective-permute-done.2.x_two_ref
  31.2 1.5 %final_step.1 = (f32[2000,128]{1,0:T(8,128)}, f32[3,4,128]{2,1,0:T(4,128)S(1)}) custom-call(f32[2000,128]{1,0:T(8,128)S(1)} %main_step.1.partial_ref, f32[1000,128]{1,0:T(8,128)S(1)} %collective-permute-done.1.x_one_ref, f32[1000,128]{1,0:T(8,128)S(1)} %collective-permute-done.2.x_two_ref, f32[2,2560]{1,0:T(2,128)S(1)} %collective-permute-done.3.y_one_ref, ...), custom_call_target="tpu_custom_call" | custom-call | flops 5120000 | bytes 4096000 | tf_op jit(solution)/shard_map/final_step/pallas_call | solution.py:386
  32.7 4.7 %psum.7 = f32[3,4,128]{2,1,0:T(4,128)} all-reduce(f32[3,4,128]{2,1,0:T(4,128)S(1)} %get-tuple-element.25), channel_id=1, replica_groups=mesh['gx'=16,'gy'=16,'col'=2] {'col'}, use_global_device_ids=true, to_apply=%region_0.0 | all-reduce | flops 1536 | bytes 12288 | tf_op jit(solution)/shard_map/psum | solution.py:433
  (4 shorter events, 0.0 us)
Async XLA Ops:
  0.6 23.8 %collective-permute-start = (f32[2000,128]{1,0:T(8,128)}, f32[2000,128]{1,0:T(8,128)S(1)}, u32[]{:S(2)}, u32[]{:S(2)}) collective-permute-start(f32[2000,128]{1,0:T(8,128)} %bitcast.13), channel_id=1, source_target_pairs={{0,1},{1,0},{2,3},{3,2},{4,5},{5,4},{6,7},{7,6},{8,9},{9,8},{10,11... | collective-permute-start | bytes 3072008 | tf_op jit(solution)/shard_map/ppermute | solution.py:430
  3.2 1.2 %copy-start = (f32[5,10,10,4,128]{4,3,2,1,0:T(4,128)S(1)}, f32[5,10,10,4,128]{4,3,2,1,0:T(4,128)}, u32[]{:S(2)}) copy-start(f32[5,10,10,4,128]{4,3,2,1,0:T(4,128)} %param.8) | copy-start | bytes 3072004
  4.4 10.8 %copy-start.2 = (f32[4,10,10]{2,0,1:T(4,128)S(1)}, f32[4,10,10]{2,0,1:T(4,128)}, u32[]{:S(2)}) copy-start(f32[4,10,10]{2,0,1:T(4,128)} %param.13) | copy-start | bytes 4804
  4.4 10.8 %copy-start.3 = (f32[4,10,10]{2,0,1:T(4,128)S(1)}, f32[4,10,10]{2,0,1:T(4,128)}, u32[]{:S(2)}) copy-start(f32[4,10,10]{2,0,1:T(4,128)} %param.14) | copy-start | bytes 4804
  4.5 10.9 %copy-start.4 = (f32[4,4,128]{2,1,0:T(4,128)S(1)}, f32[4,4,128]{2,1,0:T(4,128)}, u32[]{:S(2)}) copy-start(f32[4,4,128]{2,1,0:T(4,128)} %param.10) | copy-start | bytes 24580
  4.5 10.9 %copy-start.5 = (f32[10,10]{1,0:T(8,128)S(1)}, f32[10,10]{1,0:T(8,128)}, u32[]{:S(2)}) copy-start(f32[10,10]{1,0:T(8,128)} %refs_4_.1) | copy-start | bytes 1204
  4.5 10.9 %copy-start.6 = (f32[10,10]{1,0:T(8,128)S(1)}, f32[10,10]{1,0:T(8,128)}, u32[]{:S(2)}) copy-start(f32[10,10]{1,0:T(8,128)} %refs_5_.1) | copy-start | bytes 1204
  4.5 10.9 %copy-start.7 = (f32[2,4,128]{2,1,0:T(4,128)S(1)}, f32[2,4,128]{2,1,0:T(4,128)}, u32[]{:S(2)}) copy-start(f32[2,4,128]{2,1,0:T(4,128)} %param.9) | copy-start | bytes 12292
  4.5 19.7 %copy-start.8 = (f32[3,5,10,10]{3,0,2,1:T(4,128)S(1)}, f32[3,5,10,10]{3,0,2,1:T(4,128)}, u32[]{:S(2)}) copy-start(f32[3,5,10,10]{3,0,2,1:T(4,128)} %param.15) | copy-start | bytes 18004
  5.6 18.9 %copy-start.1 = (f32[5,10,10,4,128]{4,3,2,1,0:T(4,128)S(1)}, f32[5,10,10,4,128]{4,3,2,1,0:T(4,128)}, u32[]{:S(2)}) copy-start(f32[5,10,10,4,128]{4,3,2,1,0:T(4,128)} %param.8) | copy-start | bytes 3072004
  5.6 25.6 %collective-permute-start.1 = (f32[1000,128]{1,0:T(8,128)}, f32[1000,128]{1,0:T(8,128)S(1)}, u32[]{:S(2)}, u32[]{:S(2)}) collective-permute-start(f32[1000,128]{1,0:T(8,128)} %get-tuple-element.20), channel_id=1, source_target_pairs={{32,64},{96,128},{160,192},{224,256},{288,320},{352,384},{416,448}... | collective-permute-start | bytes 1536008 | tf_op jit(solution)/shard_map/ppermute | solution.py:423
  8.8 22.4 %collective-permute-start.2 = (f32[1000,128]{1,0:T(8,128)}, f32[1000,128]{1,0:T(8,128)S(1)}, u32[]{:S(2)}, u32[]{:S(2)}) collective-permute-start(f32[1000,128]{1,0:T(8,128)} %get-tuple-element.21), channel_id=1, source_target_pairs={{0,32},{64,96},{128,160},{192,224},{256,288},{320,352},{384,416},{... | collective-permute-start | bytes 1536008 | tf_op jit(solution)/shard_map/ppermute | solution.py:424
  15.8 12.9 %collective-permute-start.3 = (f32[2,2560]{1,0:T(2,128)S(1)}, f32[2,2560]{1,0:T(2,128)S(1)}, u32[]{:S(2)}, u32[]{:S(2)}) collective-permute-start(f32[2,2560]{1,0:T(2,128)S(1)} %get-tuple-element.22), channel_id=1, source_target_pairs={{0,2},{4,6},{8,10},{12,14},{16,18},{20,22},{24,26},{28,30},{2,0},{... | collective-permute-start | bytes 61448 | tf_op jit(solution)/shard_map/ppermute | solution.py:428
  20.6 10.5 %collective-permute-start.4 = (f32[2,2560]{1,0:T(2,128)S(1)}, f32[2,2560]{1,0:T(2,128)S(1)}, u32[]{:S(2)}, u32[]{:S(2)}) collective-permute-start(f32[2,2560]{1,0:T(2,128)S(1)} %get-tuple-element.23), channel_id=1, source_target_pairs={{2,4},{6,8},{10,12},{14,16},{18,20},{22,24},{26,28},{4,2},{8,6},{1... | collective-permute-start | bytes 61448 | tf_op jit(solution)/shard_map/ppermute | solution.py:429

commit v4 on v3

--- a/solution.py
+++ b/solution.py
@@ -51,31 +51,54 @@
     return jnp.where(condition, 1.0, 0.0).astype(f32)
 
 
-def halo_kernel(x_ref, one_ref, two_ref):
+def halo_kernel(x_hbm, one_hbm, two_hbm, x_ref, one_ref, two_ref, in_sems, out_sems):
     odd = 1 - lax.rem(lax.axis_index("gx"), 2)
-    for ref, offset in ((one_ref, 2 - 2 * odd), (two_ref, 2 * odd)):
-        for p in range(5):
+    loads = []
+    stores = []
+    for p in range(5):
+        rows = pl.ds(400 * p, 400)
+        loads.append(pltpu.make_async_copy(x_hbm.at[rows], x_ref.at[rows], in_sems.at[p]))
+        loads[p].start()
+    for p in range(5):
+        loads[p].wait()
+        layers = pl.ds(2 * MODES_P * p, 2 * MODES_P)
+        for i, (ref, target, offset) in enumerate(
+            ((one_ref, one_hbm, 2 - 2 * odd), (two_ref, two_hbm, 2 * odd))
+        ):
             for k in range(2):
-                ref[pl.ds(MODES_P * (2 * p + k), MODES_P), :] = x_ref[pl.ds(400 * p + k + offset, MODES_P, stride=4), :]
+                ref[x_halo_rows(p, k), :] = x_ref[pl.ds(400 * p + k + offset, MODES_P, stride=4), :]
+            stores.append(pltpu.make_async_copy(ref.at[layers], target.at[layers], out_sems.at[2 * p + i]))
+            stores[-1].start()
+    for store in stores:
+        store.wait()
+
+
+def x_halo_rows(p, k):
+    return pl.ds(MODES_P * (2 * p + k), MODES_P)
 
 
 def x_halos(rows):
     shape = jax.ShapeDtypeStruct((ROWS // 2, 128), f32)
+    half = pltpu.VMEM((ROWS // 2, 128), f32)
     return pl.pallas_call(
         halo_kernel,
-        in_specs=[vmem],
-        out_specs=[vmem, vmem],
+        in_specs=[hbm],
+        out_specs=[hbm, hbm],
         out_shape=[shape, shape],
+        scratch_shapes=[
+            pltpu.VMEM((ROWS, 128), f32),
+            half,
+            half,
+            pltpu.SemaphoreType.DMA((5,)),
+            pltpu.SemaphoreType.DMA((10,)),
+        ],
         cost_estimate=pl.CostEstimate(flops=0, bytes_accessed=2 * ROWS * 512, transcendentals=0),
         compiler_params=pltpu.CompilerParams(vmem_limit_bytes=16 << 20),
         name="x_halos",
-    )(rows)
-
-
-def edge_kernel(x_ref, *refs):
-    small, (one_ref, two_ref), kept, (rows_ref,) = refs[:6], refs[6:8], refs[8:14], refs[14:]
-    for source, target in zip(small, kept):
-        target[...] = source[...]
+    )(pltpu.with_memory_space_constraint(rows, pltpu.HBM))
+
+
+def edge_kernel(x_ref, one_ref, two_ref, rows_ref):
     for x in range(4):
         rows_ref[x * 128 + 96 : (x + 1) * 128, :] = jnp.zeros((32, 256), bf16)
     lane = lax.rem(iota((8, 256), 1), 128)
@@ -92,19 +115,18 @@
         two_ref[:, p * 512 : (p + 1) * 512] = edges[2:4]
 
 
-def y_edges(rows, small):
+def y_edges(rows):
     shape = jax.ShapeDtypeStruct((2, 5 * 512), f32)
-    outs = pl.pallas_call(
+    return pl.pallas_call(
         edge_kernel,
-        in_specs=[vmem] * 7,
-        out_specs=[vmem] * 8,
-        out_shape=[shape, shape] + [jax.ShapeDtypeStruct(a.shape, f32) for a in small],
+        in_specs=[vmem],
+        out_specs=[vmem, vmem],
+        out_shape=[shape, shape],
         scratch_shapes=[pltpu.VMEM((512, 256), bf16)],
         cost_estimate=pl.CostEstimate(flops=0, bytes_accessed=ROWS * 512, transcendentals=0),
         compiler_params=pltpu.CompilerParams(vmem_limit_bytes=16 << 20),
         name="y_edges",
-    )(rows, *small)
-    return outs[0], outs[1], outs[2:]
+    )(rows)
 
 
 def split(value):
@@ -319,7 +341,7 @@
     odd_y = lax.rem(lax.axis_index("gy"), 2) == 1
 
     def halo(on_left, p, k):
-        layer = pl.ds(MODES_P * (2 * p + k), MODES_P)
+        layer = x_halo_rows(p, k)
         one, two = x_one_ref[layer, :], x_two_ref[layer, :]
         return jnp.where(odd_x, one, two) if on_left else jnp.where(odd_x, two, one)
 
@@ -337,7 +359,6 @@
     hit = hit | ((row == 0) & (lane == 128))
     hit = hit | ((row == 3) & (lane == 255))
     place = one_hot(hit).astype(bf16)
-    stress = [jnp.zeros((1, 128), f32) for _ in range(12)]
     copies = []
     for p in range(5):
         lanes = slice(p * 512, (p + 1) * 512)
@@ -369,15 +390,15 @@
             if x == 3:
                 total = total + up1[3:4] * right_near + up2[3:4] * right_far
             out_ref[pl.ds(400 * p + x, MODES_P, stride=4), :] = total
-            for s in range(3):
-                moment = jnp.sum(weight_ref[p, :, s : s + 1] * total, axis=0, keepdims=True)
-                stress[4 * s + x] = stress[4 * s + x] + moment
         rows = pl.ds(400 * p, 400)
         copies.append(pltpu.make_async_copy(out_ref.at[rows], out_hbm.at[rows], sems.at[p]))
         copies[-1].start()
-    for s in range(3):
-        for x in range(4):
-            stress_ref[s, x : x + 1, :] = stress[4 * s + x]
+    for x in range(4):
+        for s in range(3):
+            moment = jnp.zeros((MODES_P, 128), f32)
+            for p in range(5):
+                moment = moment + weight_ref[p, :, s : s + 1] * out_ref[pl.ds(400 * p + x, MODES_P, stride=4), :]
+            stress_ref[s, x : x + 1, :] = jnp.sum(moment, axis=0, keepdims=True)
     for copy in copies:
         copy.wait()
 
@@ -422,9 +443,7 @@
     send_one, send_two = x_halos(rows)
     x_one = lax.ppermute(send_one, "gx", ring_one)
     x_two = lax.ppermute(send_two, "gx", ring_two)
-    small = (speeds, shear, first, second, hermite_matrix, laguerre_matrix)
-    send_one, send_two, small = y_edges(rows, small)
-    speeds, shear, first, second, hermite_matrix, laguerre_matrix = small
+    send_one, send_two = y_edges(rows)
     y_one = lax.ppermute(send_one, "gy", line_one)
     y_two = lax.ppermute(send_two, "gy", line_two)
     other = lax.ppermute(rows, "col", [(0, 1), (1, 0)])

time: 37.7 us -> 37.7 us (level)
  Pallas kernels: 7.39 us -> 8.48 us
  waiting for transfers between devices: 2.37 us -> 1.63 us
  local copies, waits for them, and re-layouts: 1.53 us -> 1 us
    pallas_call x2, Pallas kernels: 1.57 us -> 2.62 us  [the longest x1 2.13 us: x_halos(): pl.pallas_call(halo_kernel, in_specs=[hbm], out_specs=[hbm, hbm], out_sha...]
    ppermute x1, waiting for transfers between devices: 2.36 us -> 1.62 us  [body(): y_two = lax.ppermute(send_two, 'gy', line_two)]
    unnamed x19 -> x17, local copies, waits for them, and re-layouts: 1.26 us -> 0.73 us
  transfers between devices with their start and end apart: 5 -> 5, of which waited for: 1 -> 1; matrix products, arithmetic and copies ran while one was open for 1% -> 1% of each run, Pallas kernels for 16% -> 19%
where the time goes in v4:
time: 37.7 us; the launch traced here: 37.4 us
  starting transfers between devices  20.7 us (55%)
  Pallas kernels  8.48 us (22%)
  blocking collectives  4.74 us (13%)
  waiting for transfers between devices  1.63 us (4%)
  local copies, waits for them, and re-layouts  1 us (3%)
  between operations  0.8 us (2%)
    ppermute x1, starting transfers between devices, body(): x_two = lax.ppermute(send_two, 'gx', ring_two)  6.6 us
    ppermute x1, starting transfers between devices, body(): y_one = lax.ppermute(send_one, 'gy', line_one)  4.76 us
    psum x1, blocking collectives, body(): stress = lax.psum(stress, 'col')  4.74 us
    pallas_call x1, Pallas kernels, main(): pl.pallas_call(main_kernel, in_specs=[vmem] * 8, out_specs=vmem, out_shap...  4.3 us
    ppermute x1, starting transfers between devices, body(): y_two = lax.ppermute(send_two, 'gy', line_two)  3.52 us
    ppermute x1, starting transfers between devices, body(): x_one = lax.ppermute(send_one, 'gx', ring_one)  3.12 us
    ppermute x1, starting transfers between devices, body(): other = lax.ppermute(rows, 'col', [(0, 1), (1, 0)])  2.71 us
    pallas_call x1, Pallas kernels, x_halos(): pl.pallas_call(halo_kernel, in_specs=[hbm], out_specs=[hbm, hbm], out_sha...  2.13 us
  transfers between devices with their start and end apart: 5, of which 1 were waited for; matrix products, arithmetic and copies ran while one was open for 1% of the time, Pallas kernels for 19%

profile of v4, /device:TPU:259, one launch (start us, length us, event | category | flops | bytes accessed | tf_op | source)
XLA Modules:
  0.0 37.4 jit_solution(5875288414864811995)
XLA Ops:
  0.6 0.0 copy-start
  0.6 2.7 %collective-permute-start = (f32[2000,128]{1,0:T(8,128)}, f32[2000,128]{1,0:T(8,128)S(1)}, u32[]{:S(2)}, u32[]{:S(2)}) collective-permute-start(f32[2000,128]{1,0:T(8,128)} %bitcast.13), channel_id=1, source_target_pairs={{0,1},{1,0},{2,3},{3,2},{4,5},{5,4},{6,7},{7,6},{8,9},{9,8},{10,11... | collective-permute-start | bytes 3072008 | tf_op jit(solution)/shard_map/ppermute | solution.py:449
  3.4 2.1 %x_halos.1 = (f32[1000,128]{1,0:T(8,128)}, f32[1000,128]{1,0:T(8,128)}) custom-call(f32[2000,128]{1,0:T(8,128)} %bitcast.14), custom_call_target="tpu_custom_call" | custom-call | bytes 2048000 | tf_op jit(solution)/shard_map/x_halos/pallas_call | solution.py:83
  5.5 3.1 %collective-permute-start.1 = (f32[1000,128]{1,0:T(8,128)}, f32[1000,128]{1,0:T(8,128)S(1)}, u32[]{:S(2)}, u32[]{:S(2)}) collective-permute-start(f32[1000,128]{1,0:T(8,128)} %get-tuple-element.8), channel_id=1, source_target_pairs={{32,64},{96,128},{160,192},{224,256},{288,320},{352,384},{416,448}... | collective-permute-start | bytes 1536008 | tf_op jit(solution)/shard_map/ppermute | solution.py:444
  8.6 0.0 copy-start.7
  8.6 6.6 %collective-permute-start.2 = (f32[1000,128]{1,0:T(8,128)}, f32[1000,128]{1,0:T(8,128)S(1)}, u32[]{:S(2)}, u32[]{:S(2)}) collective-permute-start(f32[1000,128]{1,0:T(8,128)} %get-tuple-element.9), channel_id=1, source_target_pairs={{0,32},{64,96},{128,160},{192,224},{256,288},{320,352},{384,416},{... | collective-permute-start | bytes 1536008 | tf_op jit(solution)/shard_map/ppermute | solution.py:445
  15.2 0.0 copy-done
  15.3 0.5 %y_edges.1 = (f32[2,2560]{1,0:T(2,128)S(1)}, f32[2,2560]{1,0:T(2,128)S(1)}) custom-call(f32[2000,128]{1,0:T(8,128)S(1)} %bitcast.15), custom_call_target="tpu_custom_call" | custom-call | bytes 1024000 | tf_op jit(solution)/shard_map/y_edges/pallas_call | solution.py:120
  15.7 4.8 %collective-permute-start.3 = (f32[2,2560]{1,0:T(2,128)S(1)}, f32[2,2560]{1,0:T(2,128)S(1)}, u32[]{:S(2)}, u32[]{:S(2)}) collective-permute-start(f32[2,2560]{1,0:T(2,128)S(1)} %get-tuple-element.10), channel_id=1, source_target_pairs={{0,2},{4,6},{8,10},{12,14},{16,18},{20,22},{24,26},{28,30},{2,0},{... | collective-permute-start | bytes 61448 | tf_op jit(solution)/shard_map/ppermute | solution.py:447
  20.5 3.5 %collective-permute-start.4 = (f32[2,2560]{1,0:T(2,128)S(1)}, f32[2,2560]{1,0:T(2,128)S(1)}, u32[]{:S(2)}, u32[]{:S(2)}) collective-permute-start(f32[2,2560]{1,0:T(2,128)S(1)} %get-tuple-element.11), channel_id=1, source_target_pairs={{2,4},{6,8},{10,12},{14,16},{18,20},{22,24},{26,28},{4,2},{8,6},{1... | collective-permute-start | bytes 61448 | tf_op jit(solution)/shard_map/ppermute | solution.py:448
  24.0 0.0 copy-done.7
  24.1 0.1 reshape.30
  24.2 0.0 copy-start.2
  24.2 0.0 copy-start.3
  24.2 0.0 copy-start.4
  24.2 0.0 copy-start.5
  24.2 0.0 copy-start.6
  24.2 0.2 copy.12
  24.4 0.0 copy-start.1
  24.4 0.0 collective-permute-done.other_ref
  24.4 0.5 %copy-done.2 = f32[4,10,10]{2,0,1:T(4,128)S(1)} copy-done((f32[4,10,10]{2,0,1:T(4,128)S(1)}, f32[4,10,10]{2,0,1:T(4,128)}, u32[]{:S(2)}) %copy-start.2) | copy-done | bytes 1624
  24.9 0.0 copy-done.3
  24.9 0.0 copy-done.4
  24.9 0.0 copy-done.6
  24.9 0.2 copy-done.1
  25.1 4.3 %main_step.1.partial_ref = f32[2000,128]{1,0:T(8,128)S(1)} custom-call(f32[10,10]{1,0:T(8,128)S(1)} %copy-done.4, f32[2000,128]{1,0:T(8,128)S(1)} %bitcast.16, f32[2000,128]{1,0:T(8,128)S(1)} %collective-permute-done.other_ref, f32[8,128]{1,0:T(8,128)S(1)} %bitcast.18, f32[16,128]{1,0:T(8,128)S(1)} %bitcast.22, f32[40,10]{1,0:T(8,128)S(1)} %bitcast.20, ...), custom_call_target="tpu_custom_call" | custom-call | flops 1101004800 | bytes 3072000 | tf_op jit(solution)/shard_map/main_step/pallas_call | solution.py:307
  29.4 0.0 collective-permute-done.3.y_one_ref
  29.4 1.6 %collective-permute-done.4.y_two_ref = f32[2,2560]{1,0:T(2,128)S(1)} collective-permute-done((f32[2,2560]{1,0:T(2,128)S(1)}, f32[2,2560]{1,0:T(2,128)S(1)}, u32[]{:S(2)}, u32[]{:S(2)}) %collective-permute-start.4) | collective-permute-done | bytes 20512 | tf_op jit(solution)/shard_map/ppermute | solution.py:448
  31.1 0.0 collective-permute-done.1.x_one_ref
  31.1 0.0 collective-permute-done.2.x_two_ref
  31.1 1.6 %final_step.1 = (f32[2000,128]{1,0:T(8,128)}, f32[3,4,128]{2,1,0:T(4,128)S(1)}) custom-call(f32[2000,128]{1,0:T(8,128)S(1)} %main_step.1.partial_ref, f32[1000,128]{1,0:T(8,128)S(1)} %collective-permute-done.1.x_one_ref, f32[1000,128]{1,0:T(8,128)S(1)} %collective-permute-done.2.x_two_ref, f32[2,2560]{1,0:T(2,128)S(1)} %collective-permute-done.3.y_one_ref, ...), custom_call_target="tpu_custom_call" | custom-call | flops 5120000 | bytes 4096000 | tf_op jit(solution)/shard_map/final_step/pallas_call | solution.py:407
  32.6 4.7 %psum.7 = f32[3,4,128]{2,1,0:T(4,128)} all-reduce(f32[3,4,128]{2,1,0:T(4,128)S(1)} %get-tuple-element.13), channel_id=1, replica_groups=mesh['gx'=16,'gy'=16,'col'=2] {'col'}, use_global_device_ids=true, to_apply=%region_0.0 | all-reduce | flops 1536 | bytes 12288 | tf_op jit(solution)/shard_map/psum | solution.py:452
  (2 shorter events, 0.0 us)
Async XLA Ops:
  0.6 14.6 %copy-start = (f32[5,10,10,4,128]{4,3,2,1,0:T(4,128)S(1)}, f32[5,10,10,4,128]{4,3,2,1,0:T(4,128)}, u32[]{:S(2)}) copy-start(f32[5,10,10,4,128]{4,3,2,1,0:T(4,128)} %param.8) | copy-start | bytes 3072004
  0.6 23.8 %collective-permute-start = (f32[2000,128]{1,0:T(8,128)}, f32[2000,128]{1,0:T(8,128)S(1)}, u32[]{:S(2)}, u32[]{:S(2)}) collective-permute-start(f32[2000,128]{1,0:T(8,128)} %bitcast.13), channel_id=1, source_target_pairs={{0,1},{1,0},{2,3},{3,2},{4,5},{5,4},{6,7},{7,6},{8,9},{9,8},{10,11... | collective-permute-start | bytes 3072008 | tf_op jit(solution)/shard_map/ppermute | solution.py:449
  5.5 25.6 %collective-permute-start.1 = (f32[1000,128]{1,0:T(8,128)}, f32[1000,128]{1,0:T(8,128)S(1)}, u32[]{:S(2)}, u32[]{:S(2)}) collective-permute-start(f32[1000,128]{1,0:T(8,128)} %get-tuple-element.8), channel_id=1, source_target_pairs={{32,64},{96,128},{160,192},{224,256},{288,320},{352,384},{416,448}... | collective-permute-start | bytes 1536008 | tf_op jit(solution)/shard_map/ppermute | solution.py:444
  8.6 15.4 %copy-start.7 = (f32[3,5,10,10]{3,0,2,1:T(4,128)S(1)}, f32[3,5,10,10]{3,0,2,1:T(4,128)}, u32[]{:S(2)}) copy-start(f32[3,5,10,10]{3,0,2,1:T(4,128)} %param.15) | copy-start | bytes 18004
  8.6 22.4 %collective-permute-start.2 = (f32[1000,128]{1,0:T(8,128)}, f32[1000,128]{1,0:T(8,128)S(1)}, u32[]{:S(2)}, u32[]{:S(2)}) collective-permute-start(f32[1000,128]{1,0:T(8,128)} %get-tuple-element.9), channel_id=1, source_target_pairs={{0,32},{64,96},{128,160},{192,224},{256,288},{320,352},{384,416},{... | collective-permute-start | bytes 1536008 | tf_op jit(solution)/shard_map/ppermute | solution.py:445
  15.7 13.7 %collective-permute-start.3 = (f32[2,2560]{1,0:T(2,128)S(1)}, f32[2,2560]{1,0:T(2,128)S(1)}, u32[]{:S(2)}, u32[]{:S(2)}) collective-permute-start(f32[2,2560]{1,0:T(2,128)S(1)} %get-tuple-element.10), channel_id=1, source_target_pairs={{0,2},{4,6},{8,10},{12,14},{16,18},{20,22},{24,26},{28,30},{2,0},{... | collective-permute-start | bytes 61448 | tf_op jit(solution)/shard_map/ppermute | solution.py:447
  20.5 10.5 %collective-permute-start.4 = (f32[2,2560]{1,0:T(2,128)S(1)}, f32[2,2560]{1,0:T(2,128)S(1)}, u32[]{:S(2)}, u32[]{:S(2)}) collective-permute-start(f32[2,2560]{1,0:T(2,128)S(1)} %get-tuple-element.11), channel_id=1, source_target_pairs={{2,4},{6,8},{10,12},{14,16},{18,20},{22,24},{26,28},{4,2},{8,6},{1... | collective-permute-start | bytes 61448 | tf_op jit(solution)/shard_map/ppermute | solution.py:448
  24.2 0.7 %copy-start.2 = (f32[4,10,10]{2,0,1:T(4,128)S(1)}, f32[4,10,10]{2,0,1:T(4,128)}, u32[]{:S(2)}) copy-start(f32[4,10,10]{2,0,1:T(4,128)} %param.13) | copy-start | bytes 4804
  24.2 0.7 %copy-start.3 = (f32[4,10,10]{2,0,1:T(4,128)S(1)}, f32[4,10,10]{2,0,1:T(4,128)}, u32[]{:S(2)}) copy-start(f32[4,10,10]{2,0,1:T(4,128)} %param.14) | copy-start | bytes 4804
  24.2 0.7 %copy-start.4 = (f32[10,10]{1,0:T(8,128)S(1)}, f32[10,10]{1,0:T(8,128)}, u32[]{:S(2)}) copy-start(f32[10,10]{1,0:T(8,128)} %laguerre_ref.1) | copy-start | bytes 1204
  24.2 0.7 %copy-start.5 = (f32[4,4,128]{2,1,0:T(4,128)S(1)}, f32[4,4,128]{2,1,0:T(4,128)}, u32[]{:S(2)}) copy-start(f32[4,4,128]{2,1,0:T(4,128)} %param.10) | copy-start | bytes 24580
  24.2 0.7 %copy-start.6 = (f32[10,10]{1,0:T(8,128)S(1)}, f32[10,10]{1,0:T(8,128)}, u32[]{:S(2)}) copy-start(f32[10,10]{1,0:T(8,128)} %hermite_ref.1) | copy-start | bytes 1204
  24.4 0.7 %copy-start.1 = (f32[2,4,128]{2,1,0:T(4,128)S(1)}, f32[2,4,128]{2,1,0:T(4,128)}, u32[]{:S(2)}) copy-start(f32[2,4,128]{2,1,0:T(4,128)} %param.9) | copy-start | bytes 12292

commit v5 on v3

--- a/solution.py
+++ b/solution.py
@@ -72,10 +72,7 @@
     )(rows)
 
 
-def edge_kernel(x_ref, *refs):
-    small, (one_ref, two_ref), kept, (rows_ref,) = refs[:6], refs[6:8], refs[8:14], refs[14:]
-    for source, target in zip(small, kept):
-        target[...] = source[...]
+def edge_kernel(x_ref, one_ref, two_ref, rows_ref):
     for x in range(4):
         rows_ref[x * 128 + 96 : (x + 1) * 128, :] = jnp.zeros((32, 256), bf16)
     lane = lax.rem(iota((8, 256), 1), 128)
@@ -92,19 +89,18 @@
         two_ref[:, p * 512 : (p + 1) * 512] = edges[2:4]
 
 
-def y_edges(rows, small):
+def y_edges(rows):
     shape = jax.ShapeDtypeStruct((2, 5 * 512), f32)
-    outs = pl.pallas_call(
+    return pl.pallas_call(
         edge_kernel,
-        in_specs=[vmem] * 7,
-        out_specs=[vmem] * 8,
-        out_shape=[shape, shape] + [jax.ShapeDtypeStruct(a.shape, f32) for a in small],
+        in_specs=[vmem],
+        out_specs=[vmem, vmem],
+        out_shape=[shape, shape],
         scratch_shapes=[pltpu.VMEM((512, 256), bf16)],
         cost_estimate=pl.CostEstimate(flops=0, bytes_accessed=ROWS * 512, transcendentals=0),
         compiler_params=pltpu.CompilerParams(vmem_limit_bytes=16 << 20),
         name="y_edges",
-    )(rows, *small)
-    return outs[0], outs[1], outs[2:]
+    )(rows)
 
 
 def split(value):
@@ -422,9 +418,7 @@
     send_one, send_two = x_halos(rows)
     x_one = lax.ppermute(send_one, "gx", ring_one)
     x_two = lax.ppermute(send_two, "gx", ring_two)
-    small = (speeds, shear, first, second, hermite_matrix, laguerre_matrix)
-    send_one, send_two, small = y_edges(rows, small)
-    speeds, shear, first, second, hermite_matrix, laguerre_matrix = small
+    send_one, send_two = y_edges(rows)
     y_one = lax.ppermute(send_one, "gy", line_one)
     y_two = lax.ppermute(send_two, "gy", line_two)
     other = lax.ppermute(rows, "col", [(0, 1), (1, 0)])

time: 37.7 us -> 37.6 us (level)
  waiting for transfers between devices: 2.37 us -> 1.63 us
  local copies, waits for them, and re-layouts: 1.53 us -> 2.2 us
    ppermute x1, waiting for transfers between devices: 2.36 us -> 1.62 us  [body(): y_two = lax.ppermute(send_two, 'gy', line_two)]
    unnamed x19, local copies, waits for them, and re-layouts: 1.26 us -> 1.93 us
where the time goes in v5:
time: 37.6 us; the launch traced here: 37.3 us
  starting transfers between devices  20.6 us (55%)
  Pallas kernels  7.37 us (20%)
  blocking collectives  4.74 us (13%)
  local copies, waits for them, and re-layouts  2.2 us (6%)
  waiting for transfers between devices  1.63 us (4%)
  between operations  0.79 us (2%)
    ppermute x1, starting transfers between devices, body(): x_two = lax.ppermute(send_two, 'gx', ring_two)  6.47 us
    ppermute x1, starting transfers between devices, body(): y_one = lax.ppermute(send_one, 'gy', line_one)  4.76 us
    psum x1, blocking collectives, body(): stress = lax.psum(stress, 'col')  4.74 us
    pallas_call x1, Pallas kernels, main(): pl.pallas_call(main_kernel, in_specs=[vmem] * 8, out_specs=vmem, out_shap...  4.31 us
    ppermute x1, starting transfers between devices, body(): y_two = lax.ppermute(send_two, 'gy', line_two)  3.52 us
    ppermute x1, starting transfers between devices, body(): x_one = lax.ppermute(send_one, 'gx', ring_one)  3.24 us
    ppermute x1, starting transfers between devices, body(): other = lax.ppermute(rows, 'col', [(0, 1), (1, 0)])  2.59 us
    unnamed x19, local copies, waits for them, and re-layouts  1.93 us
  transfers between devices with their start and end apart: 5, of which 1 were waited for; matrix products, arithmetic and copies ran while one was open for 1% of the time, Pallas kernels for 16%

profile of v5, /device:TPU:259, one launch (start us, length us, event | category | flops | bytes accessed | tf_op | source)
XLA Modules:
  0.0 37.3 jit_solution(9493974546238250894)
XLA Ops:
  0.6 2.6 %collective-permute-start = (f32[2000,128]{1,0:T(8,128)}, f32[2000,128]{1,0:T(8,128)S(1)}, u32[]{:S(2)}, u32[]{:S(2)}) collective-permute-start(f32[2000,128]{1,0:T(8,128)} %bitcast.13), channel_id=1, source_target_pairs={{0,1},{1,0},{2,3},{3,2},{4,5},{5,4},{6,7},{7,6},{8,9},{9,8},{10,11... | collective-permute-start | bytes 3072008 | tf_op jit(solution)/shard_map/ppermute | solution.py:424
  3.2 0.0 copy-start
  3.2 1.2 %copy-done = f32[5,10,10,4,128]{4,3,2,1,0:T(4,128)S(1)} copy-done((f32[5,10,10,4,128]{4,3,2,1,0:T(4,128)S(1)}, f32[5,10,10,4,128]{4,3,2,1,0:T(4,128)}, u32[]{:S(2)}) %copy-start) | copy-done | bytes 1024024
  4.4 1.1 %x_halos.1 = (f32[1000,128]{1,0:T(8,128)}, f32[1000,128]{1,0:T(8,128)}) custom-call(f32[2000,128]{1,0:T(8,128)S(1)} %bitcast.14), custom_call_target="tpu_custom_call" | custom-call | bytes 2048000 | tf_op jit(solution)/shard_map/x_halos/pallas_call | solution.py:64
  5.5 3.2 %collective-permute-start.1 = (f32[1000,128]{1,0:T(8,128)}, f32[1000,128]{1,0:T(8,128)S(1)}, u32[]{:S(2)}, u32[]{:S(2)}) collective-permute-start(f32[1000,128]{1,0:T(8,128)} %get-tuple-element.8), channel_id=1, source_target_pairs={{32,64},{96,128},{160,192},{224,256},{288,320},{352,384},{416,448}... | collective-permute-start | bytes 1536008 | tf_op jit(solution)/shard_map/ppermute | solution.py:419
  8.8 6.5 %collective-permute-start.2 = (f32[1000,128]{1,0:T(8,128)}, f32[1000,128]{1,0:T(8,128)S(1)}, u32[]{:S(2)}, u32[]{:S(2)}) collective-permute-start(f32[1000,128]{1,0:T(8,128)} %get-tuple-element.9), channel_id=1, source_target_pairs={{0,32},{64,96},{128,160},{192,224},{256,288},{320,352},{384,416},{... | collective-permute-start | bytes 1536008 | tf_op jit(solution)/shard_map/ppermute | solution.py:420
  15.2 0.5 %y_edges.1 = (f32[2,2560]{1,0:T(2,128)S(1)}, f32[2,2560]{1,0:T(2,128)S(1)}) custom-call(f32[2000,128]{1,0:T(8,128)S(1)} %bitcast.15), custom_call_target="tpu_custom_call" | custom-call | bytes 1024000 | tf_op jit(solution)/shard_map/y_edges/pallas_call | solution.py:94
  15.7 4.8 %collective-permute-start.3 = (f32[2,2560]{1,0:T(2,128)S(1)}, f32[2,2560]{1,0:T(2,128)S(1)}, u32[]{:S(2)}, u32[]{:S(2)}) collective-permute-start(f32[2,2560]{1,0:T(2,128)S(1)} %get-tuple-element.10), channel_id=1, source_target_pairs={{0,2},{4,6},{8,10},{12,14},{16,18},{20,22},{24,26},{28,30},{2,0},{... | collective-permute-start | bytes 61448 | tf_op jit(solution)/shard_map/ppermute | solution.py:422
  20.5 3.5 %collective-permute-start.4 = (f32[2,2560]{1,0:T(2,128)S(1)}, f32[2,2560]{1,0:T(2,128)S(1)}, u32[]{:S(2)}, u32[]{:S(2)}) collective-permute-start(f32[2,2560]{1,0:T(2,128)S(1)} %get-tuple-element.11), channel_id=1, source_target_pairs={{2,4},{6,8},{10,12},{14,16},{18,20},{22,24},{26,28},{4,2},{8,6},{1... | collective-permute-start | bytes 61448 | tf_op jit(solution)/shard_map/ppermute | solution.py:423
  24.0 0.0 copy-done.8
  24.1 0.1 reshape.30
  24.2 0.0 copy-start.3
  24.2 0.0 copy-start.4
  24.2 0.0 copy-start.5
  24.2 0.0 copy-start.6
  24.2 0.0 copy-start.7
  24.2 0.2 copy.12
  24.4 0.0 copy-start.2
  24.4 0.0 collective-permute-done.other_ref
  24.4 0.0 copy-done.1
  24.4 0.5 %copy-done.3 = f32[4,10,10]{2,0,1:T(4,128)S(1)} copy-done((f32[4,10,10]{2,0,1:T(4,128)S(1)}, f32[4,10,10]{2,0,1:T(4,128)}, u32[]{:S(2)}) %copy-start.3) | copy-done | bytes 1624
  24.9 0.0 copy-done.4
  24.9 0.0 copy-done.6
  24.9 0.0 copy-done.7
  24.9 0.2 copy-done.2
  25.1 4.3 %main_step.1.partial_ref = f32[2000,128]{1,0:T(8,128)S(1)} custom-call(f32[10,10]{1,0:T(8,128)S(1)} %copy-done.5, f32[2000,128]{1,0:T(8,128)S(1)} %bitcast.16, f32[2000,128]{1,0:T(8,128)S(1)} %collective-permute-done.other_ref, f32[8,128]{1,0:T(8,128)S(1)} %bitcast.18, f32[16,128]{1,0:T(8,128)S(1)} %bitcast.22, f32[40,10]{1,0:T(8,128)S(1)} %bitcast.20, ...), custom_call_target="tpu_custom_call" | custom-call | flops 1101004800 | bytes 3072000 | tf_op jit(solution)/shard_map/main_step/pallas_call | solution.py:281
  29.4 0.0 collective-permute-done.3.y_one_ref
  29.4 1.6 %collective-permute-done.4.y_two_ref = f32[2,2560]{1,0:T(2,128)S(1)} collective-permute-done((f32[2,2560]{1,0:T(2,128)S(1)}, f32[2,2560]{1,0:T(2,128)S(1)}, u32[]{:S(2)}, u32[]{:S(2)}) %collective-permute-start.4) | collective-permute-done | bytes 20512 | tf_op jit(solution)/shard_map/ppermute | solution.py:423
  31.0 0.0 collective-permute-done.1.x_one_ref
  31.0 0.0 collective-permute-done.2.x_two_ref
  31.0 1.5 %final_step.1 = (f32[2000,128]{1,0:T(8,128)}, f32[3,4,128]{2,1,0:T(4,128)S(1)}) custom-call(f32[2000,128]{1,0:T(8,128)S(1)} %main_step.1.partial_ref, f32[1000,128]{1,0:T(8,128)S(1)} %collective-permute-done.1.x_one_ref, f32[1000,128]{1,0:T(8,128)S(1)} %collective-permute-done.2.x_two_ref, f32[2,2560]{1,0:T(2,128)S(1)} %collective-permute-done.3.y_one_ref, ...), custom_call_target="tpu_custom_call" | custom-call | flops 5120000 | bytes 4096000 | tf_op jit(solution)/shard_map/final_step/pallas_call | solution.py:382
  32.6 4.7 %psum.7 = f32[3,4,128]{2,1,0:T(4,128)} all-reduce(f32[3,4,128]{2,1,0:T(4,128)S(1)} %get-tuple-element.13), channel_id=1, replica_groups=mesh['gx'=16,'gy'=16,'col'=2] {'col'}, use_global_device_ids=true, to_apply=%region_0.0 | all-reduce | flops 1536 | bytes 12288 | tf_op jit(solution)/shard_map/psum | solution.py:427
  (4 shorter events, 0.0 us)
Async XLA Ops:
  0.6 23.8 %collective-permute-start = (f32[2000,128]{1,0:T(8,128)}, f32[2000,128]{1,0:T(8,128)S(1)}, u32[]{:S(2)}, u32[]{:S(2)}) collective-permute-start(f32[2000,128]{1,0:T(8,128)} %bitcast.13), channel_id=1, source_target_pairs={{0,1},{1,0},{2,3},{3,2},{4,5},{5,4},{6,7},{7,6},{8,9},{9,8},{10,11... | collective-permute-start | bytes 3072008 | tf_op jit(solution)/shard_map/ppermute | solution.py:424
  3.2 1.2 %copy-start = (f32[5,10,10,4,128]{4,3,2,1,0:T(4,128)S(1)}, f32[5,10,10,4,128]{4,3,2,1,0:T(4,128)}, u32[]{:S(2)}) copy-start(f32[5,10,10,4,128]{4,3,2,1,0:T(4,128)} %param.8) | copy-start | bytes 3072004
  4.4 19.6 %copy-start.8 = (f32[3,5,10,10]{3,0,2,1:T(4,128)S(1)}, f32[3,5,10,10]{3,0,2,1:T(4,128)}, u32[]{:S(2)}) copy-start(f32[3,5,10,10]{3,0,2,1:T(4,128)} %param.15) | copy-start | bytes 18004
  5.5 18.9 %copy-start.1 = (f32[5,10,10,4,128]{4,3,2,1,0:T(4,128)S(1)}, f32[5,10,10,4,128]{4,3,2,1,0:T(4,128)}, u32[]{:S(2)}) copy-start(f32[5,10,10,4,128]{4,3,2,1,0:T(4,128)} %param.8) | copy-start | bytes 3072004
  5.5 25.5 %collective-permute-start.1 = (f32[1000,128]{1,0:T(8,128)}, f32[1000,128]{1,0:T(8,128)S(1)}, u32[]{:S(2)}, u32[]{:S(2)}) collective-permute-start(f32[1000,128]{1,0:T(8,128)} %get-tuple-element.8), channel_id=1, source_target_pairs={{32,64},{96,128},{160,192},{224,256},{288,320},{352,384},{416,448}... | collective-permute-start | bytes 1536008 | tf_op jit(solution)/shard_map/ppermute | solution.py:419
  8.8 22.3 %collective-permute-start.2 = (f32[1000,128]{1,0:T(8,128)}, f32[1000,128]{1,0:T(8,128)S(1)}, u32[]{:S(2)}, u32[]{:S(2)}) collective-permute-start(f32[1000,128]{1,0:T(8,128)} %get-tuple-element.9), channel_id=1, source_target_pairs={{0,32},{64,96},{128,160},{192,224},{256,288},{320,352},{384,416},{... | collective-permute-start | bytes 1536008 | tf_op jit(solution)/shard_map/ppermute | solution.py:420
  15.7 13.7 %collective-permute-start.3 = (f32[2,2560]{1,0:T(2,128)S(1)}, f32[2,2560]{1,0:T(2,128)S(1)}, u32[]{:S(2)}, u32[]{:S(2)}) collective-permute-start(f32[2,2560]{1,0:T(2,128)S(1)} %get-tuple-element.10), channel_id=1, source_target_pairs={{0,2},{4,6},{8,10},{12,14},{16,18},{20,22},{24,26},{28,30},{2,0},{... | collective-permute-start | bytes 61448 | tf_op jit(solution)/shard_map/ppermute | solution.py:422
  20.5 10.5 %collective-permute-start.4 = (f32[2,2560]{1,0:T(2,128)S(1)}, f32[2,2560]{1,0:T(2,128)S(1)}, u32[]{:S(2)}, u32[]{:S(2)}) collective-permute-start(f32[2,2560]{1,0:T(2,128)S(1)} %get-tuple-element.11), channel_id=1, source_target_pairs={{2,4},{6,8},{10,12},{14,16},{18,20},{22,24},{26,28},{4,2},{8,6},{1... | collective-permute-start | bytes 61448 | tf_op jit(solution)/shard_map/ppermute | solution.py:423
  24.2 0.7 %copy-start.3 = (f32[4,10,10]{2,0,1:T(4,128)S(1)}, f32[4,10,10]{2,0,1:T(4,128)}, u32[]{:S(2)}) copy-start(f32[4,10,10]{2,0,1:T(4,128)} %param.13) | copy-start | bytes 4804
  24.2 0.7 %copy-start.4 = (f32[4,10,10]{2,0,1:T(4,128)S(1)}, f32[4,10,10]{2,0,1:T(4,128)}, u32[]{:S(2)}) copy-start(f32[4,10,10]{2,0,1:T(4,128)} %param.14) | copy-start | bytes 4804
  24.2 0.7 %copy-start.5 = (f32[10,10]{1,0:T(8,128)S(1)}, f32[10,10]{1,0:T(8,128)}, u32[]{:S(2)}) copy-start(f32[10,10]{1,0:T(8,128)} %laguerre_ref.1) | copy-start | bytes 1204
  24.2 0.7 %copy-start.6 = (f32[4,4,128]{2,1,0:T(4,128)S(1)}, f32[4,4,128]{2,1,0:T(4,128)}, u32[]{:S(2)}) copy-start(f32[4,4,128]{2,1,0:T(4,128)} %param.10) | copy-start | bytes 24580
  24.2 0.7 %copy-start.7 = (f32[10,10]{1,0:T(8,128)S(1)}, f32[10,10]{1,0:T(8,128)}, u32[]{:S(2)}) copy-start(f32[10,10]{1,0:T(8,128)} %hermite_ref.1) | copy-start | bytes 1204
  24.4 0.7 %copy-start.2 = (f32[2,4,128]{2,1,0:T(4,128)S(1)}, f32[2,4,128]{2,1,0:T(4,128)}, u32[]{:S(2)}) copy-start(f32[2,4,128]{2,1,0:T(4,128)} %param.9) | copy-start | bytes 12292
